TPU v7x, 768 devices: a whole 4x8x12 slice. The times are simulated.
768 devices in a mesh: dom: 96 (over y, z), sub: 8 (over x, core).
Axes of the slice: x: 4, y: 8, z: 12, core: 2. Of those that a mesh axis runs over, the one named last changes fastest.
Arguments:
- coarse_state: float32 [9, 64, 98304], P(None, None, ('dom', 'sub')), may hold values from -6 to 6
- fine_nodal_state: float32 [9, 64, 98304], P(None, None, ('dom', 'sub')), may hold values from -6 to 6
- coarse_elastic: float32 [2, 98304], P(None, ('dom', 'sub')), may hold values from 1.2 to 4.8
- coarse_density: float32 [98304], P(('dom', 'sub')), may hold values from 0.5 to 1
- fine_lame_shear: float32 [2, 98304], P(None, ('dom', 'sub')), may hold values from 1.2 to 4.8
- fine_density: float32 [98304], P(('dom', 'sub')), may hold values from 0.5 to 1
- coarse_links: int32 [6, 98304], P(None, ('dom', 'sub')), may hold values from 0 to 383, as said below
- fine_links: int32 [6, 98304], P(None, ('dom', 'sub')), may hold values from 0 to 383, as said below
- coarse_send: int32 [98304], P(('dom', 'sub')), may hold values from 0 to 767, as said below
- fine_return: int32 [98304], P(('dom', 'sub')), may hold values from 0 to 767, as said below
- source_elem: int32 [3072], P(('dom', 'sub')), may hold values from 0 to 127
- source_amp: float32 [9, 3072], P(None, ('dom', 'sub')), may hold values from -6 to 6
- source_shape: float32 [64, 3072], P(None, ('dom', 'sub')), may hold values from -60 to 60
Outputs:
- coarse_final: float32 [9, 64, 98304], P(None, None, ('dom', 'sub'))
- fine_final: float32 [9, 64, 98304], P(None, None, ('dom', 'sub'))
Inputs may be any that keep to these rules, and one draw needn't show every extreme that they name: `coarse_links`: entry (f, e) of a device's block names the element whose trace meets face f of local element e: local elements first, then 64 of the device below and 64 of the device above along dom+sub, then interface slot k at 256 + k. Slot k = b * 16 + s is read for slots b that device b returns. `fine_links`: as for coarse_links; slot k = a 16 + s holds what device a of the group sent. `coarse_send`: Face-major local face index for slot k = b * 16 + s toward sub index b; distinct within a device. `fine_return`: Face-major local face index for slot k = a 16 + s toward sub index a; distinct within a device.
All inputs are finite; a program needn't handle non-finite values.
Results may differ from a plain program's by a relative error of at most 0.0003.
Values sent between devices are 32-bit elements; how exact they have to be, the bound alone decides.
A program may use at most 64 MiB of HBM per device.

v0:
```python
import math

import jax
import jax.numpy as jnp
import numpy as np
from jax import lax
from jax.sharding import PartitionSpec as P

ORDER = 4
LAYERS = 2
SUBSTEPS = 2


highest_order = lax.Precision.HIGHEST
coarse_dt = 0.03
coarse_scale = 1.0
fine_scale = 2.0
lift_weight = 6.0


def padded(cells, sides, width):
    for axis, dim in sides:
        count = lax.axis_size(axis)
        head = lax.slice_in_dim(cells, 0, width, axis=dim)
        tail = lax.slice_in_dim(cells, cells.shape[dim] - width, cells.shape[dim], axis=dim)
        cells = jnp.concatenate(
            [
                lax.ppermute(tail, axis, [(i, (i + 1) % count) for i in range(count)]),
                cells,
                lax.ppermute(head, axis, [((i + 1) % count, i) for i in range(count)]),
            ],
            axis=dim,
        )
    return cells


def derivative_tables():
    points = np.array([-1.0, -1.0 / math.sqrt(5.0), 1.0 / math.sqrt(5.0), 1.0])
    barycentric = np.array(
        [
            1.0
            / np.prod(
                [
                    points[col_index] - points[other_index]
                    for other_index in range(4)
                    if other_index != col_index
                ]
            )
            for col_index in range(4)
        ]
    )
    derivative = np.zeros((4, 4))
    for row_index in range(4):
        for col_index in range(4):
            if row_index != col_index:
                derivative[row_index, col_index] = (
                    barycentric[col_index]
                    / barycentric[row_index]
                    / (points[row_index] - points[col_index])
                )
        derivative[row_index, row_index] = -np.sum(derivative[row_index])
    eye_four = np.eye(4)
    along_x = np.kron(derivative, np.eye(16))
    along_y = np.kron(np.kron(eye_four, derivative), eye_four)
    along_z = np.kron(np.eye(16), derivative)
    return np.stack([along_x, along_y, along_z])


def make_material(elastic, density):
    lame = elastic[0]
    shear = elastic[1]
    buoyancy = 1.0 / density
    speed = jnp.sqrt((lame + 2.0 * shear) * buoyancy)
    return (lame, shear, buoyancy, speed)


def stress_rates(grad_x, grad_y, grad_z, material):
    lame, shear, buoyancy = (material[0], material[1], material[2])
    spread = grad_x[6] + grad_y[7] + grad_z[8]
    rates = [
        lame * spread + 2.0 * shear * grad_x[6],
        lame * spread + 2.0 * shear * grad_y[7],
        lame * spread + 2.0 * shear * grad_z[8],
        shear * (grad_y[6] + grad_x[7]),
        shear * (grad_z[7] + grad_y[8]),
        shear * (grad_z[6] + grad_x[8]),
        buoyancy * (grad_x[0] + grad_y[3] + grad_z[5]),
        buoyancy * (grad_x[3] + grad_y[1] + grad_z[4]),
        buoyancy * (grad_x[5] + grad_y[4] + grad_z[2]),
    ]
    return jnp.stack(rates)


def volume_rate(nodal_field, material, gradient_scale):
    lookup_tables = jnp.asarray(derivative_tables(), jnp.float32)
    spatial_gradients = (
        jnp.einsum("ygq,kqp->ykgp", lookup_tables, nodal_field, precision=highest_order)
        * gradient_scale
    )
    return stress_rates(spatial_gradients[0], spatial_gradients[1], spatial_gradients[2], material)


def face_traces(nodal_field):
    count_elems = nodal_field.shape[-1]
    cube = nodal_field.reshape(9, 4, 4, 4, count_elems)
    slices = [
        cube[:, 0],
        cube[:, 3],
        cube[:, :, 0],
        cube[:, :, 3],
        cube[:, :, :, 0],
        cube[:, :, :, 3],
    ]
    return [piece.reshape(144, count_elems) for piece in slices]


def lift_faces(volume, corrections):
    count_elems = volume.shape[-1]
    shaped = [piece.reshape(9, 4, 4, count_elems) for piece in corrections]
    zero_face = jnp.zeros_like(shaped[0])
    along_first = jnp.stack([shaped[0], zero_face, zero_face, shaped[1]], axis=1)
    along_second = jnp.stack([shaped[2], zero_face, zero_face, shaped[3]], axis=2)
    along_third = jnp.stack([shaped[4], zero_face, zero_face, shaped[5]], axis=3)
    cube = volume.reshape(9, 4, 4, 4, count_elems) + along_first + along_second + along_third
    return cube.reshape(9, 64, count_elems)


def predict(nodal_field, material, gradient_scale):
    terms = [nodal_field]
    for order_index in range(ORDER - 1):
        terms.append(volume_rate(terms[-1], material, gradient_scale))
    return terms


def taylor(terms, start, stop):
    total = None
    for order_index in range(len(terms)):
        weight = (stop ** (order_index + 1) - start ** (order_index + 1)) / math.factorial(
            order_index + 1
        )
        total = (
            terms[order_index] * weight if total is None else total + terms[order_index] * weight
        )
    return total


def halo_source(traces):
    count_elems = traces[0].shape[1]
    lower_half = jnp.arange(count_elems)[None, :] < count_elems // 2
    return jnp.where(lower_half, traces[4], traces[5])


def correct(
    nodal_field,
    integral,
    traces,
    material,
    links,
    halo_lower,
    halo_upper,
    interface,
    gradient_scale,
):
    volume_change = volume_rate(integral, material, gradient_scale)
    zero_trace = jnp.zeros_like(traces[0]).reshape(9, 16, -1)
    corrections = []
    for face_index in range(6):
        trace_table = jnp.concatenate(
            [traces[face_index ^ 1], halo_lower, halo_upper, interface], axis=1
        )
        outer_trace = jnp.take(trace_table, links[face_index], axis=1)
        jump_trace = (outer_trace - traces[face_index]).reshape(9, 16, -1)
        signed = jump_trace if face_index % 2 else -jump_trace
        spatial_gradients = [zero_trace, zero_trace, zero_trace]
        spatial_gradients[face_index // 2] = signed
        normal = stress_rates(
            spatial_gradients[0], spatial_gradients[1], spatial_gradients[2], material
        )
        corrections.append(
            ((normal + material[3] * jump_trace) * (0.5 * lift_weight * gradient_scale)).reshape(
                144, -1
            )
        )
    return lift_faces(nodal_field + volume_change, corrections)


def face_columns(nodal_field, columns):
    return jnp.take(jnp.concatenate(face_traces(nodal_field), axis=1), columns, axis=1)


def source_field(source_elem, source_amp, source_shape, count_elems):
    onehot = (source_elem[:, None] == jnp.arange(count_elems)[None, :]).astype(jnp.float32)
    pattern = (source_amp[:, None, :] * source_shape[None, :, :]).reshape(9 * 64, -1)
    return (coarse_dt * jnp.dot(pattern, onehot, precision=highest_order)).reshape(
        9, 64, count_elems
    )


def advance(nodal_field, integral, material, links, interface, gradient_scale):
    traces = face_traces(integral)
    count_elems = nodal_field.shape[-1]
    layer_width = count_elems // LAYERS
    extended = padded(halo_source(traces), ((("dom", "sub"), 1),), layer_width)
    halo_lower = extended[:, :layer_width]
    halo_upper = extended[:, layer_width + count_elems :]
    return correct(
        nodal_field,
        integral,
        traces,
        material,
        links,
        halo_lower,
        halo_upper,
        interface,
        gradient_scale,
    )


def per_device(
    coarse_state,
    fine_nodal_state,
    coarse_elastic,
    coarse_density,
    fine_lame_shear,
    fine_density,
    coarse_links,
    fine_links,
    coarse_send,
    fine_return,
    source_elem,
    source_amp,
    source_shape,
):
    fine_dt = coarse_dt / SUBSTEPS
    count_elems = coarse_state.shape[-1]
    coarse_material = make_material(coarse_elastic, coarse_density)
    fine_material = make_material(fine_lame_shear, fine_density)
    sources = source_field(source_elem, source_amp, source_shape, count_elems)
    coarse_field = coarse_state
    fine_field = fine_nodal_state
    coarse_terms = predict(coarse_field, coarse_material, coarse_scale)
    coarse_integral = taylor(coarse_terms, 0.0, coarse_dt)
    outgoing = jnp.stack([face_columns(term_field, coarse_send) for term_field in coarse_terms])
    incoming = lax.all_to_all(outgoing, "sub", split_axis=2, concat_axis=2, tiled=True)
    returned = None
    for sub_index in range(SUBSTEPS):
        interface = taylor(
            [incoming[order_index] for order_index in range(ORDER)],
            sub_index * fine_dt,
            (sub_index + 1) * fine_dt,
        )
        fine_terms = predict(fine_field, fine_material, fine_scale)
        fine_integral = taylor(fine_terms, 0.0, fine_dt)
        fine_field = advance(
            fine_field, fine_integral, fine_material, fine_links, interface, fine_scale
        )
        piece_back = face_columns(fine_integral, fine_return)
        piece_back = lax.all_to_all(piece_back, "sub", split_axis=1, concat_axis=1, tiled=True)
        returned = piece_back if returned is None else returned + piece_back
    coarse_field = (
        advance(
            coarse_field, coarse_integral, coarse_material, coarse_links, returned, coarse_scale
        )
        + sources
    )
    return (coarse_field, fine_field)


def solution(mesh):
    return jax.shard_map(
        per_device,
        mesh=mesh,
        in_specs=(
            P(None, None, ("dom", "sub")),
            P(None, None, ("dom", "sub")),
            P(None, ("dom", "sub")),
            P(("dom", "sub")),
            P(None, ("dom", "sub")),
            P(("dom", "sub")),
            P(None, ("dom", "sub")),
            P(None, ("dom", "sub")),
            P(("dom", "sub")),
            P(("dom", "sub")),
            P(("dom", "sub")),
            P(None, ("dom", "sub")),
            P(None, ("dom", "sub")),
        ),
        out_specs=(P(None, None, ("dom", "sub")), P(None, None, ("dom", "sub"))),
        check_vma=False,
    )
```

profile of v0, /device:TPU:1, one launch (start us, length us, event | category | flops | bytes accessed | tf_op | source)
XLA Modules:
  0.0 217.9 jit_solution(9135236484280738068)
XLA Ops:
  1.4 0.9 fusion.216
  6.5 0.9 convolution_bitcast_fusion.1
  19.7 0.9 copy-done.92
  25.6 0.9 copy-done.88
  29.8 0.9 constant_dynamic-update-slice_fusion.98
  31.4 0.9 copy-done.59
  32.3 0.9 copy-done.60
  33.2 0.9 copy-done.56
  34.1 0.9 copy-done.57
  35.0 1.4 gather_fusion.1
  36.4 0.9 constant_dynamic-update-slice_fusion.97
  37.4 0.9 copy-done.66
  38.3 0.9 copy-done.64
  39.2 0.9 copy-done.65
  40.1 1.4 gather_fusion.2
  41.5 0.9 constant_dynamic-update-slice_fusion.113
  42.5 0.9 copy-done.63
  43.4 0.9 copy-done.61
  44.3 0.9 copy-done.54
  45.2 0.9 copy-done.55
  48.1 1.1 copy.1023
  49.2 14.0 %all-to-all-start.1 = ((f32[4,144,128]{1,0,2:T(4,128)}), f32[4,144,128]{1,0,2:T(4,128)S(1)}, u32[]{:S(2)}, u32[]{:S(2)}) async-start(f32[4,144,128]{1,0,2:T(4,128)} %copy.1023), calls=%async_computation.1 | async-start | bytes 1048576 | tf_op jit(solution)/shard_map/all_to_all | solution.py:244
  66.2 0.9 fusion.6
  67.2 0.8 fusion.5
  74.5 3.5 %collective-permute-start.2 = (f32[144,64]{0,1:T(8,128)}, f32[144,64]{0,1:T(8,128)}, u32[]{:S(2)}, u32[]{:S(2)}) collective-permute-start(f32[144,64]{0,1:T(8,128)} %get-tuple-element.185), channel_id=1, source_target_pairs={{0,1},{1,2},{2,3},{3,4},{4,5},{5,6},{6,7},{7,8},{8,9},{9,10},{10,1... | collective-permute-start | bytes 110600 | tf_op jit(solution)/shard_map/ppermute | solution.py:28
  78.0 2.1 collective-permute-start.3
  83.1 0.9 fusion.4
  98.4 2.6 %gather_fusion = f32[128,144]{1,0:T(8,128)} fusion(f32[144,768]{0,1:T(8,128)} %get-tuple-element.188, s32[1024]{0:T(1024)} %get-tuple-element.543), kind=kCustom, calls=%fused_computation.clone | custom fusion | bytes 147968 | tf_op jit(solution)/shard_map/jit(_take)/gather | solution.py:188
  101.7 1.0 convolution_multiply_fusion.8
  104.1 0.9 pad_maximum_fusion.37
  108.2 1.0 pad_maximum_fusion.41
  110.9 0.9 copy-done.37
  116.0 0.9 copy-done.25
  117.0 0.9 gather_fusion.7
  118.8 0.9 gather_fusion.8
  125.1 0.8 fusion.3
  126.1 0.8 fusion.2
  127.1 0.9 fusion.1
  128.4 0.9 fusion
  134.6 3.6 %collective-permute-start.4 = (f32[144,64]{0,1:T(8,128)}, f32[144,64]{0,1:T(8,128)S(1)}, u32[]{:S(2)}, u32[]{:S(2)}) collective-permute-start(f32[144,64]{0,1:T(8,128)} %get-tuple-element.179), channel_id=1, source_target_pairs={{0,1},{1,2},{2,3},{3,4},{4,5},{5,6},{6,7},{7,8},{8,9},{9,10},{10,1... | collective-permute-start | bytes 110600 | tf_op jit(solution)/shard_map/ppermute | solution.py:28
  138.2 8.4 %collective-permute-start.5 = (f32[144,64]{0,1:T(8,128)}, f32[144,64]{0,1:T(8,128)S(1)}, u32[]{:S(2)}, u32[]{:S(2)}) collective-permute-start(f32[144,64]{0,1:T(8,128)} %get-tuple-element.180), channel_id=1, source_target_pairs={{1,0},{2,1},{3,2},{4,3},{5,4},{6,5},{7,6},{8,7},{9,8},{10,9},{11,1... | collective-permute-start | bytes 110600 | tf_op jit(solution)/shard_map/ppermute | solution.py:30
  146.7 2.0 gather_fusion.11
  149.6 10.6 %all-to-all-start = ((f32[144,8,16]{0,2,1:T(8,128)}), f32[144,8,16]{0,2,1:T(8,128)S(1)}, u32[]{:S(2)}, u32[]{:S(2)}) async-start(f32[144,8,16]{0,2,1:T(8,128)} %bitcast.99), calls=%async_computation | async-start | bytes 262144 | tf_op jit(solution)/shard_map/all_to_all | solution.py:258
  160.8 3.5 %collective-permute-start = (f32[144,64]{0,1:T(8,128)}, f32[144,64]{0,1:T(8,128)}, u32[]{:S(2)}, u32[]{:S(2)}) collective-permute-start(f32[144,64]{0,1:T(8,128)} %get-tuple-element.183), channel_id=1, source_target_pairs={{0,1},{1,2},{2,3},{3,4},{4,5},{5,6},{6,7},{7,8},{8,9},{9,10},{10,1... | collective-permute-start | bytes 110600 | tf_op jit(solution)/shard_map/ppermute | solution.py:28
  164.4 2.1 collective-permute-start.1
  169.2 0.9 gather_fusion.22
  171.4 0.9 gather_fusion.23
  173.8 0.9 gather_fusion.18
  175.4 0.9 copy-done.111
  176.3 0.9 gather_fusion.19
  178.0 0.9 gather_fusion.20
  179.5 0.9 gather_fusion.21
  183.2 8.9 %all-to-all-start.2 = ((f32[144,8,16]{0,2,1:T(8,128)}), f32[144,8,16]{0,2,1:T(8,128)S(1)}, u32[]{:S(2)}, u32[]{:S(2)}) async-start(f32[144,8,16]{0,2,1:T(8,128)} %bitcast.304), calls=%async_computation.2 | async-start | bytes 262144 | tf_op jit(solution)/shard_map/all_to_all | solution.py:258
  192.8 4.6 %all-to-all-done.2 = f32[144,8,16]{0,2,1:T(8,128)S(1)} async-done(((f32[144,8,16]{0,2,1:T(8,128)}), f32[144,8,16]{0,2,1:T(8,128)S(1)}, u32[]{:S(2)}, u32[]{:S(2)}) %all-to-all-start.2) | async-done | bytes 73760 | tf_op jit(solution)/shard_map/all_to_all | solution.py:258
  197.4 0.9 pad_maximum_fusion.43
  198.3 0.9 gather_fusion.16
  199.3 1.0 gather_fusion.17
  201.3 1.0 pad_maximum_fusion.47
  202.3 0.9 gather_fusion.12
  204.1 0.9 copy-done.31
  205.7 0.9 gather_fusion.13
  207.5 0.9 copy-done.19
  208.5 0.9 gather_fusion.14
  210.3 0.9 gather_fusion.15
  (805 shorter events, 100.1 us)
Async XLA Ops:
  0.6 1.7 copy-start.1
  2.5 1.9 copy-start
  3.8 4.7 %copy-start.98 = (f32[128]{0:T(128)}, f32[128]{0:T(128)S(1)}, u32[]{:S(2)}) copy-start(f32[128]{0:T(128)S(1)} %get-tuple-element.466) | copy-start | bytes 1540
  3.8 4.7 %copy-start.108 = (f32[128]{0:T(128)}, f32[128]{0:T(128)S(1)}, u32[]{:S(2)}) copy-start(f32[128]{0:T(128)S(1)} %get-tuple-element.467) | copy-start | bytes 1540
  3.8 4.9 %copy-start.95 = (f32[128]{0:T(128)}, f32[128]{0:T(128)S(1)}, u32[]{:S(2)}) copy-start(f32[128]{0:T(128)S(1)} %get-tuple-element.465) | copy-start | bytes 1540
  4.4 4.4 %copy-start.101 = (f32[128]{0:T(128)}, f32[128]{0:T(128)S(1)}, u32[]{:S(2)}) copy-start(f32[128]{0:T(128)S(1)} %get-tuple-element.452) | copy-start | bytes 1540
  29.8 1.6 copy-start.58
  36.4 1.0 copy-start.67
  41.5 1.0 copy-start.62
  47.0 0.9 copy-start.79
  47.0 1.0 copy-start.80
  49.2 15.9 %copy-start.2 = (f32[9,64,128]{2,1,0:T(8,128)S(1)}, f32[9,64,128]{2,1,0:T(8,128)}, u32[]{:S(2)}) copy-start(f32[9,64,128]{2,1,0:T(8,128)} %param.30) | copy-start | bytes 884740
  49.2 53.5 %all-to-all-start.1 = ((f32[4,144,128]{1,0,2:T(4,128)}), f32[4,144,128]{1,0,2:T(4,128)S(1)}, u32[]{:S(2)}, u32[]{:S(2)}) async-start(f32[4,144,128]{1,0,2:T(4,128)} %copy.1023), calls=%async_computation.1 | async-start | bytes 1048576 | tf_op jit(solution)/shard_map/all_to_all | solution.py:244
  63.9 9.2 %copy-start.143 = (pred[128]{0:T(512)(128)(4,1)}, pred[128]{0:T(512)(128)(4,1)S(1)}, u32[]{:S(2)}) copy-start(pred[128]{0:T(512)(128)(4,1)S(1)} %iota_compare_fusion.2) | copy-start | bytes 388
  64.6 3.5 %copy-start.112 = (f32[128]{0:T(128)}, f32[128]{0:T(128)S(1)}, u32[]{:S(2)}) copy-start(f32[128]{0:T(128)S(1)} %get-tuple-element.464) | copy-start | bytes 1540
  64.6 3.5 %copy-start.43 = (f32[128]{0:T(128)}, f32[128]{0:T(128)S(1)}, u32[]{:S(2)}) copy-start(f32[128]{0:T(128)S(1)} %get-tuple-element.463) | copy-start | bytes 1540
  64.6 3.6 %copy-start.40 = (f32[128]{0:T(128)}, f32[128]{0:T(128)S(1)}, u32[]{:S(2)}) copy-start(f32[128]{0:T(128)S(1)} %get-tuple-element.462) | copy-start | bytes 1540
  65.2 3.0 %copy-start.46 = (f32[128]{0:T(128)}, f32[128]{0:T(128)S(1)}, u32[]{:S(2)}) copy-start(f32[128]{0:T(128)S(1)} %get-tuple-element.456) | copy-start | bytes 1540
  68.6 1.0 copy-start.22
  69.2 1.2 copy-start.9
  69.4 3.7 %copy-start.5 = (f32[144,128]{0,1:T(8,128)}, f32[144,128]{0,1:T(8,128)S(1)}, u32[]{:S(2)}) copy-start(f32[144,128]{0,1:T(8,128)S(1)} %copy.941) | copy-start | bytes 221188
  69.6 1.5 copy-start.11
  69.7 2.0 copy-start.13
  73.1 7.5 %copy-start.75 = (f32[9,64,128]{2,1,0:T(8,128)S(1)}, f32[9,64,128]{2,1,0:T(8,128)}, u32[]{:S(2)}) copy-start(f32[9,64,128]{2,1,0:T(8,128)} %copy-done.74) | copy-start | bytes 884740
  74.5 28.8 %collective-permute-start.2 = (f32[144,64]{0,1:T(8,128)}, f32[144,64]{0,1:T(8,128)}, u32[]{:S(2)}, u32[]{:S(2)}) collective-permute-start(f32[144,64]{0,1:T(8,128)} %get-tuple-element.185), channel_id=1, source_target_pairs={{0,1},{1,2},{2,3},{3,4},{4,5},{5,6},{6,7},{7,8},{8,9},{9,10},{10,1... | collective-permute-start | bytes 110600 | tf_op jit(solution)/shard_map/ppermute | solution.py:28
  78.0 25.2 %collective-permute-start.3 = (f32[144,64]{0,1:T(8,128)}, f32[144,64]{0,1:T(8,128)}, u32[]{:S(2)}, u32[]{:S(2)}) collective-permute-start(f32[144,64]{0,1:T(8,128)} %get-tuple-element.186), channel_id=1, source_target_pairs={{1,0},{2,1},{3,2},{4,3},{5,4},{6,5},{7,6},{8,7},{9,8},{10,9},{11,1... | collective-permute-start | bytes 110600 | tf_op jit(solution)/shard_map/ppermute | solution.py:30
  80.8 12.0 %copy-start.16 = (f32[9,4,1,4,128]{4,3,2,1,0:T(4,128)}, f32[9,4,1,4,128]{4,3,2,1,0:T(4,128)S(1)}, u32[]{:S(2)}) copy-start(f32[9,4,1,4,128]{4,3,2,1,0:T(4,128)S(1)} %get-tuple-element.122) | copy-start | bytes 221188
  80.8 12.7 %copy-start.28 = (f32[9,4,1,4,128]{4,3,2,1,0:T(4,128)}, f32[9,4,1,4,128]{4,3,2,1,0:T(4,128)S(1)}, u32[]{:S(2)}) copy-start(f32[9,4,1,4,128]{4,3,2,1,0:T(4,128)S(1)} %get-tuple-element.121) | copy-start | bytes 221188
  90.2 3.3 %copy-start.70 = (f32[9,64,128]{2,1,0:T(8,128)}, f32[9,64,128]{2,1,0:T(8,128)S(1)}, u32[]{:S(2)}) copy-start(f32[9,64,128]{2,1,0:T(8,128)S(1)} %constant_dynamic-update-slice_fusion.69) | copy-start | bytes 884740
  90.2 19.0 %copy-start.124 = (s32[1024]{0:T(1024)}, s32[1024]{0:T(1024)S(1)}, u32[]{:S(2)}) copy-start(s32[1024]{0:T(1024)S(1)} %get-tuple-element.541) | copy-start | bytes 12292
  90.2 24.1 %copy-start.123 = (s32[1024]{0:T(1024)}, s32[1024]{0:T(1024)S(1)}, u32[]{:S(2)}) copy-start(s32[1024]{0:T(1024)S(1)} %get-tuple-element.540) | copy-start | bytes 12292
  90.9 14.1 %copy-start.126 = (s32[1024]{0:T(1024)}, s32[1024]{0:T(1024)S(1)}, u32[]{:S(2)}) copy-start(s32[1024]{0:T(1024)S(1)} %get-tuple-element.537) | copy-start | bytes 12292
  90.9 15.6 %copy-start.125 = (s32[1024]{0:T(1024)}, s32[1024]{0:T(1024)S(1)}, u32[]{:S(2)}) copy-start(s32[1024]{0:T(1024)S(1)} %get-tuple-element.536) | copy-start | bytes 12292
  95.4 37.8 %copy-start.3 = (f32[144,128]{0,1:T(8,128)}, f32[144,128]{0,1:T(8,128)S(1)}, u32[]{:S(2)}) copy-start(f32[144,128]{0,1:T(8,128)S(1)} %copy.926) | copy-start | bytes 221188
  103.1 0.9 copy-start.6
  106.5 1.5 copy-start.10
  106.5 1.5 copy-start.12
  106.5 1.5 copy-start.14
  107.2 1.0 copy-start.8
  110.0 0.9 copy-start.85
  115.1 0.9 copy-start.83
  124.0 1.0 copy-start.71
  134.6 33.3 %collective-permute-start.4 = (f32[144,64]{0,1:T(8,128)}, f32[144,64]{0,1:T(8,128)S(1)}, u32[]{:S(2)}, u32[]{:S(2)}) collective-permute-start(f32[144,64]{0,1:T(8,128)} %get-tuple-element.179), channel_id=1, source_target_pairs={{0,1},{1,2},{2,3},{3,4},{4,5},{5,6},{6,7},{7,8},{8,9},{9,10},{10,1... | collective-permute-start | bytes 110600 | tf_op jit(solution)/shard_map/ppermute | solution.py:28
  138.2 29.7 %collective-permute-start.5 = (f32[144,64]{0,1:T(8,128)}, f32[144,64]{0,1:T(8,128)S(1)}, u32[]{:S(2)}, u32[]{:S(2)}) collective-permute-start(f32[144,64]{0,1:T(8,128)} %get-tuple-element.180), channel_id=1, source_target_pairs={{1,0},{2,1},{3,2},{4,3},{5,4},{6,5},{7,6},{8,7},{9,8},{10,9},{11,1... | collective-permute-start | bytes 110600 | tf_op jit(solution)/shard_map/ppermute | solution.py:30
  146.7 2.1 copy-start.78
  146.7 2.1 copy-start.153
  149.6 10.6 %copy-start.53 = (f32[144,128]{0,1:T(8,128)S(1)}, f32[144,128]{0,1:T(8,128)}, u32[]{:S(2)}) copy-start(f32[144,128]{0,1:T(8,128)} %get-tuple-element.486) | copy-start | bytes 221188
  149.6 33.6 %all-to-all-start = ((f32[144,8,16]{0,2,1:T(8,128)}), f32[144,8,16]{0,2,1:T(8,128)S(1)}, u32[]{:S(2)}, u32[]{:S(2)}) async-start(f32[144,8,16]{0,2,1:T(8,128)} %bitcast.99), calls=%async_computation | async-start | bytes 262144 | tf_op jit(solution)/shard_map/all_to_all | solution.py:258
  160.8 36.6 %collective-permute-start = (f32[144,64]{0,1:T(8,128)}, f32[144,64]{0,1:T(8,128)}, u32[]{:S(2)}, u32[]{:S(2)}) collective-permute-start(f32[144,64]{0,1:T(8,128)} %get-tuple-element.183), channel_id=1, source_target_pairs={{0,1},{1,2},{2,3},{3,4},{4,5},{5,6},{6,7},{7,8},{8,9},{9,10},{10,1... | collective-permute-start | bytes 110600 | tf_op jit(solution)/shard_map/ppermute | solution.py:28
  164.4 33.0 %collective-permute-start.1 = (f32[144,64]{0,1:T(8,128)}, f32[144,64]{0,1:T(8,128)}, u32[]{:S(2)}, u32[]{:S(2)}) collective-permute-start(f32[144,64]{0,1:T(8,128)} %get-tuple-element.184), channel_id=1, source_target_pairs={{1,0},{2,1},{3,2},{4,3},{5,4},{6,5},{7,6},{8,7},{9,8},{10,9},{11,1... | collective-permute-start | bytes 110600 | tf_op jit(solution)/shard_map/ppermute | solution.py:30
  173.7 4.2 %copy-start.68 = (f32[144,128]{1,0:T(8,128)}, f32[144,128]{1,0:T(8,128)S(1)}, u32[]{:S(2)}) copy-start(f32[144,128]{1,0:T(8,128)S(1)} %bitcast_subtract_fusion) | copy-start | bytes 221188
  181.5 0.9 copy-start.94
  183.2 14.2 %all-to-all-start.2 = ((f32[144,8,16]{0,2,1:T(8,128)}), f32[144,8,16]{0,2,1:T(8,128)S(1)}, u32[]{:S(2)}, u32[]{:S(2)}) async-start(f32[144,8,16]{0,2,1:T(8,128)} %bitcast.304), calls=%async_computation.2 | async-start | bytes 262144 | tf_op jit(solution)/shard_map/all_to_all | solution.py:258
  192.8 4.6 %copy-start.4 = (f32[144,128]{0,1:T(8,128)S(1)}, f32[144,128]{0,1:T(8,128)}, u32[]{:S(2)}) copy-start(f32[144,128]{0,1:T(8,128)} %copy-done.3) | copy-start | bytes 221188
  199.3 1.1 copy-start.50
  199.3 1.1 copy-start.51
  199.3 1.1 copy-start.52
  200.3 0.9 copy-start.49
  202.3 2.7 %copy-start.110 = (f32[128]{0:T(128)S(1)}, f32[128]{0:T(128)}, u32[]{:S(2)}) copy-start(f32[128]{0:T(128)} %copy-done.108) | copy-start | bytes 1540
  202.3 2.7 %copy-start.120 = (f32[128]{0:T(128)S(1)}, f32[128]{0:T(128)}, u32[]{:S(2)}) copy-start(f32[128]{0:T(128)} %get-tuple-element.450) | copy-start | bytes 1540
  214.0 0.9 copy-start.82
  214.9 1.0 copy-start.73
  215.9 1.0 copy-start.15
  215.9 1.2 copy-start.77
  (104 other events, 81.1 us)
where the time goes:
time: 221 us; the launch traced here: 218 us
  local copies, waits for them, and re-layouts  120 us (54%)
  starting transfers between devices  56.9 us (26%)
  other arithmetic  20.6 us (9%)
  matrix products  11.2 us (5%)
  waiting for transfers between devices  4.58 us (2%)
  between operations  4.15 us (2%)
    unnamed x485, local copies, waits for them, and re-layouts  64.1 us
    all_to_all x2, starting transfers between devices, per_device(): lax.all_to_all(piece_back, 'sub', split_axis=1, concat_axis=1, tiled=True)  19.5 us
    gather x36, local copies, waits for them, and re-layouts, correct(): outer_trace = jnp.take(trace_table, links[face_index], axis=1)  18.3 us
    another operation x42, local copies, waits for them, and re-layouts, face_traces(): return [piece.reshape(144, count_elems) for piece in slices]  17.9 us
    all_to_all x1, starting transfers between devices, per_device(): lax.all_to_all(outgoing, 'sub', split_axis=2, concat_axis=2, tiled=True)  14 us
    ppermute x3, starting transfers between devices, padded(): lax.ppermute(head, axis, [((i + 1) % count, i) for i in range(count)])  12.7 us
    ppermute x3, starting transfers between devices, padded(): lax.ppermute(tail, axis, [(i, (i + 1) % count) for i in range(count)])  10.7 us
    dot_general x12, matrix products, volume_rate(): jnp.einsum('ygq,kqp->ykgp', lookup_tables, nodal_field, precision=highest...  10.2 us
  transfers between devices with their start and end apart: 9, of which 1 were waited for; matrix products, arithmetic and copies ran while one was open for 17% of the time, Pallas kernels for 0%

commit v1 on v0

v1 whole, which is shorter than its diff:
```python
import math

import jax
import jax.numpy as jnp
import numpy as np
from jax import lax
from jax.experimental import pallas as pl
from jax.experimental.pallas import tpu as pltpu
from jax.sharding import PartitionSpec as P

MESH = pl.DeviceIdType.MESH
COARSE_DT = 0.03
FINE_DT = 0.015
F32 = jnp.float32
BF16 = jnp.bfloat16


def derivative_tables():
    points = np.array([-1.0, -1.0 / math.sqrt(5.0), 1.0 / math.sqrt(5.0), 1.0])
    bary = np.array([1.0 / np.prod([points[c] - points[o] for o in range(4) if o != c]) for c in range(4)])
    d = np.zeros((4, 4))
    for r in range(4):
        for c in range(4):
            if r != c:
                d[r, c] = bary[c] / bary[r] / (points[r] - points[c])
        d[r, r] = -np.sum(d[r])
    eye = np.eye(4)
    along_x = np.kron(d, np.eye(16))
    along_y = np.kron(np.kron(eye, d), eye)
    along_z = np.kron(np.eye(16), d)
    full = np.concatenate([along_x, along_y, along_z]).astype(np.float32)
    high = full.astype(BF16)
    low = (full - high.astype(np.float32)).astype(BF16)
    return np.concatenate([high, low, high], axis=1)


def kernel(n_dom, n_sub, *refs):
    (qc_hbm, qf_hbm, cel, cden, fel, fden, clinks, flinks, csend, fret, selem, samp, sshape, dmat,
     outc_hbm, outf_hbm,
     qc, qf, cur, ic, if_, c0, base_c, base_f, rhs, grads, tc, t0, tf, jc, jf, tab_h, tab_i, ret0,
     hs, hr, xs, xr, in_sem, out_sem, hs_sem, hr_sem, xs_sem, xr_sem) = refs

    dom, sub = lax.axis_index("dom"), lax.axis_index("sub")
    n_all = n_dom * n_sub
    here = dom * n_sub + sub
    above, below = lax.rem(here + 1, n_all), lax.rem(here + n_all - 1, n_all)
    above_id = (above // n_sub, lax.rem(above, n_sub))
    below_id = (below // n_sub, lax.rem(below, n_sub))

    load_f = pltpu.make_async_copy(qf_hbm, qf, in_sem.at[0])
    load_c = pltpu.make_async_copy(qc_hbm, qc, in_sem.at[1])
    load_f.start()
    load_c.start()

    barrier = pltpu.get_barrier_semaphore()
    for d in range(1, n_sub):
        pl.semaphore_signal(barrier, inc=1, device_id=(dom, lax.rem(sub + d, n_sub)), device_id_type=MESH)
    for peer in (above_id, below_id):
        pl.semaphore_signal(barrier, inc=1, device_id=peer, device_id_type=MESH)

    lane = lax.broadcasted_iota(jnp.int32, (1, 128), 1)
    lane_lo = lane < 64
    sub_lo = lax.broadcasted_iota(jnp.int32, (8, 1), 0) < 4

    def material(el, den, g):
        lame, shear = el[0:1, :], el[1:2, :]
        buoy = 1.0 / den[...].reshape(1, 128)
        speed = jnp.sqrt((lame + 2.0 * shear) * buoy)
        return lame * g, shear * g, buoy * g, speed * g

    mat_c, mat_f = material(cel, cden, 1.0), material(fel, fden, 2.0)

    def rates(src, mat, emit):
        for v in range(9):
            x = src[64 * v : 64 * v + 64, :]
            high = x.astype(BF16)
            low = (x - high.astype(F32)).astype(BF16)
            at = slice(128 * v, 128 * v + 128)
            rhs[0:64, at] = high
            rhs[64:128, at] = high
            rhs[128:192, at] = low
        grads[...] = jnp.dot(dmat[...], rhs[...], preferred_element_type=F32)
        lame, shear, buoy, _ = mat

        def gr(axis, v):
            return grads[64 * axis : 64 * axis + 64, 128 * v : 128 * v + 128]

        x6, y7, z8 = gr(0, 6), gr(1, 7), gr(2, 8)
        spread = lame * (x6 + y7 + z8)
        shear2 = 2.0 * shear
        emit(0, spread + shear2 * x6)
        emit(1, spread + shear2 * y7)
        emit(2, spread + shear2 * z8)
        emit(3, shear * (gr(1, 6) + gr(0, 7)))
        emit(4, shear * (gr(2, 7) + gr(1, 8)))
        emit(5, shear * (gr(2, 6) + gr(0, 8)))
        emit(6, buoy * (gr(0, 0) + gr(1, 3) + gr(2, 5)))
        emit(7, buoy * (gr(0, 3) + gr(1, 1) + gr(2, 4)))
        emit(8, buoy * (gr(0, 5) + gr(1, 4) + gr(2, 2)))

    def predictor(src, mat, targets):
        cur[...] = src[...]
        for ref, dt in targets:
            ref[...] = src[...] * dt

        def order(k, weights):
            shrink = jnp.where(k == 0, 1.0 / 2.0, jnp.where(k == 1, 1.0 / 3.0, 1.0 / 4.0)).astype(F32)
            weights = tuple(w * (shrink * dt) for w, (_, dt) in zip(weights, targets))

            def emit(v, value):
                at = slice(64 * v, 64 * v + 64)
                cur[at, :] = value
                for (ref, _), w in zip(targets, weights):
                    ref[at, :] = ref[at, :] + w * value

            rates(cur, mat, emit)
            return weights

        lax.fori_loop(0, 3, order, tuple(jnp.float32(dt) for _, dt in targets))

    def traces(src, out):
        for v in range(9):
            out[16 * v : 16 * v + 16, :] = src[64 * v : 64 * v + 16, :]
            out[144 + 16 * v : 160 + 16 * v, :] = src[64 * v + 48 : 64 * v + 64, :]
        blocks = src[...].reshape(18, 2, 16, 128)
        even, odd = blocks[:, 0, 0:8], blocks[:, 1, 0:8]
        out[288:432, :] = jnp.where(sub_lo[None], even, pltpu.roll(odd, 4, 1)).reshape(144, 128)
        even, odd = blocks[:, 0, 8:16], blocks[:, 1, 8:16]
        out[432:576, :] = jnp.where(sub_lo[None], pltpu.roll(even, 4, 1), odd).reshape(144, 128)
        out[576:720, :] = src[pl.ds(0, 144, stride=4), :]
        out[720:864, :] = src[pl.ds(3, 144, stride=4), :]

    def gather(table, index):
        return jnp.take_along_axis(table, jnp.broadcast_to(index, table.shape), axis=1, mode="promise_in_bounds")

    def face(ref, f):
        return ref[144 * f : 144 * f + 144, :]

    def face_columns(ref, columns):
        index, which = columns & 127, columns >> 7
        total = gather(face(ref, 0), index)
        for f in range(1, 6):
            total = jnp.where(which == f, gather(face(ref, f), index), total)
        return total

    block = lane >> 4

    def butterfly(parts):
        for step in (1, 2, 4):
            keep = (block & step) == 0
            fresh = list(parts)
            for i in range(8):
                if not i & step:
                    low, high = parts[i], parts[i + step]
                    fresh[i] = jnp.where(keep, low, pltpu.roll(high, 16 * step, 1))
                    fresh[i + step] = jnp.where(keep, pltpu.roll(low, 128 - 16 * step, 1), high)
            parts = fresh
        return parts

    def exchange_copy(phase, d):
        peer = lax.rem(sub + d, n_sub)
        return pltpu.make_async_remote_copy(
            src_ref=xs.at[phase, peer], dst_ref=xr.at[phase, sub],
            send_sem=xs_sem.at[phase, d - 1], recv_sem=xr_sem.at[phase, d - 1],
            device_id=(dom, peer), device_id_type=MESH)

    def exchange_start(phase, value):
        parts = [value[24 * i : 24 * i + 24, :] for i in range(6)]
        parts = butterfly(parts + [parts[0], parts[0]])
        for b in range(8):
            xs[phase, b] = parts[b]
        for d in range(1, n_sub):
            exchange_copy(phase, d).start()

    def exchange_wait(phase):
        for d in range(1, n_sub):
            origin = lax.rem(sub + n_sub - d, n_sub)
            pltpu.make_async_remote_copy(
                src_ref=xs.at[phase, origin], dst_ref=xr.at[phase, origin],
                send_sem=xs_sem.at[phase, d - 1], recv_sem=xr_sem.at[phase, d - 1],
                device_id=(dom, origin), device_id_type=MESH).wait_recv()

    def exchange_read(phase):
        xr[phase, sub] = xs[phase, sub]
        parts = butterfly([xr[phase, a] for a in range(8)])
        return jnp.concatenate(parts[:6], axis=0)

    def halo_copies(phase):
        return [
            pltpu.make_async_remote_copy(
                src_ref=hs.at[phase, way], dst_ref=hr.at[phase, way],
                send_sem=hs_sem.at[phase, way], recv_sem=hr_sem.at[phase, way],
                device_id=peer, device_id_type=MESH)
            for way, peer in enumerate((above_id, below_id))]

    def halo_pack(phase, ref):
        low, high = ref[720:792, :], ref[792:864, :]
        hs[phase, 0] = jnp.where(lane_lo, pltpu.roll(low, 64, 1), high)
        low, high = ref[576:648, :], ref[648:720, :]
        hs[phase, 1] = jnp.where(lane_lo, low, pltpu.roll(high, 64, 1))

    def halo_start(phase):
        for copy in halo_copies(phase):
            copy.start()

    def halo_wait(phase):
        for copy in halo_copies(phase):
            copy.wait_recv()

    def halo_read(phase):
        lower, upper = hr[phase, 0], hr[phase, 1]
        tab_h[0:72, :] = jnp.where(lane_lo, lower, pltpu.roll(upper, 64, 1))
        tab_h[72:144, :] = jnp.where(lane_lo, pltpu.roll(lower, 64, 1), upper)

    def pick(links, f, table, low):
        row = links[f : f + 1, :]
        hit = (row >= low) & (row < low + 128)
        return jnp.where(hit, gather(table, row & 127), 0.0)

    def jump_own(links, t, j):
        for f in range(6):
            j[144 * f : 144 * f + 144, :] = pick(links, f, face(t, f ^ 1), 0) - face(t, f)

    def jump_add(links, j, table, low):
        for f in range(6):
            j[144 * f : 144 * f + 144, :] = face(j, f) + pick(links, f, table[...], low)

    def lift(mat, j, base, extra):
        lame, shear, buoy, speed = [3.0 * m for m in mat]
        full = lame + 2.0 * shear
        normal = (6, 7, 8)
        stress = ((0, 3, 5), (3, 1, 4), (5, 4, 2))
        for f in range(6):
            axis, sign = f // 2, 1.0 if f % 2 else -1.0
            jump = face(j, f)
            for links, table, low in extra:
                jump = jump + pick(links, f, table[...], low)
            part = [jump[16 * v : 16 * v + 16, :] for v in range(9)]
            vel = part[normal[axis]]
            lam_s, full_s, shear_s, buoy_s = sign * lame, sign * full, sign * shear, sign * buoy
            out = [None] * 9
            for v in range(3):
                out[v] = speed * part[v] + (full_s if v == axis else lam_s) * vel
            pairs = {3: (0, 1), 4: (1, 2), 5: (0, 2)}
            for v, (a, b) in pairs.items():
                out[v] = speed * part[v]
                if axis in (a, b):
                    out[v] = out[v] + shear_s * part[6 + (b if axis == a else a)]
            for v in range(3):
                out[6 + v] = speed * part[6 + v] + buoy_s * part[stress[axis][v]]
            if axis == 0:
                for v in range(9):
                    at = slice(64 * v + 48 * (f % 2), 64 * v + 48 * (f % 2) + 16)
                    base[at, :] = base[at, :] + out[v]
            elif axis == 1:
                for v in range(9):
                    for p in range(2):
                        c = out[v][8 * p : 8 * p + 8, :]
                        r = pltpu.roll(c, 4, 0)
                        at = 64 * v + 32 * p + 8 * (f % 2)
                        if f % 2:
                            first, second = jnp.where(sub_lo, 0.0, r), jnp.where(sub_lo, 0.0, c)
                        else:
                            first, second = jnp.where(sub_lo, c, 0.0), jnp.where(sub_lo, r, 0.0)
                        base[at : at + 8, :] = base[at : at + 8, :] + first
                        base[at + 16 : at + 24, :] = base[at + 16 : at + 24, :] + second
            else:
                for v in range(9):
                    at = pl.ds(64 * v + 3 * (f % 2), 16, stride=4)
                    base[at, :] = base[at, :] + out[v]

    def start_base(q, integral, mat, base):
        def emit(v, value):
            at = slice(64 * v, 64 * v + 64)
            base[at, :] = q[at, :] + value

        rates(integral, mat, emit)

    send_row = csend[...].reshape(1, 128)
    return_row = fret[...].reshape(1, 128)

    load_f.wait()
    predictor(qf, mat_f, ((if_, FINE_DT),))
    traces(if_, tf)
    halo_pack(0, tf)
    pl.semaphore_wait(barrier, n_sub + 1)
    halo_start(0)

    load_c.wait()
    predictor(qc, mat_c, ((c0, FINE_DT), (ic, COARSE_DT)))
    traces(c0, t0)
    first = face_columns(t0, send_row)
    exchange_start(0, first)

    traces(ic, tc)
    second = face_columns(tc, send_row) - first
    halo_pack(1, tc)
    start_base(qf, if_, mat_f, base_f)
    jump_own(flinks, tf, jf)
    ret0[...] = face_columns(tf, return_row)

    halo_wait(0)
    halo_read(0)
    exchange_wait(0)
    tab_i[...] = exchange_read(0)
    exchange_start(1, second)
    halo_start(1)
    lift(mat_f, jf, base_f, ((flinks, tab_h, 128), (flinks, tab_i, 256)))

    predictor(base_f, mat_f, ((if_, FINE_DT),))
    traces(if_, tf)
    halo_pack(2, tf)
    halo_start(2)
    exchange_start(2, ret0[...] + face_columns(tf, return_row))

    start_base(base_f, if_, mat_f, qf)
    jump_own(flinks, tf, jf)
    start_base(qc, ic, mat_c, base_c)
    jump_own(clinks, tc, jc)
    node_of = sshape[...]
    rows = lax.broadcasted_iota(jnp.int32, (4, 128), 0)
    lanes = lax.broadcasted_iota(jnp.int32, (4, 128), 1)
    for v in range(9):
        spots = jnp.zeros((4, 128), F32)
        for i in range(4):
            spots = jnp.where((rows == i) & (lanes == selem[i]), COARSE_DT * samp[i, v], spots)
        field = lax.dot_general(node_of, spots, (((0,), (0,)), ((), ())), precision=lax.Precision.HIGHEST,
                                preferred_element_type=F32)
        base_c[64 * v : 64 * v + 64, :] = base_c[64 * v : 64 * v + 64, :] + field
    exchange_wait(1)
    tab_i[...] = exchange_read(1)
    jump_add(flinks, jf, tab_i, 256)
    halo_wait(1)
    halo_read(1)
    jump_add(clinks, jc, tab_h, 128)

    exchange_wait(2)
    tab_i[...] = exchange_read(2)
    lift(mat_c, jc, base_c, ((clinks, tab_i, 256),))
    store_c = pltpu.make_async_copy(base_c, outc_hbm, out_sem.at[0])
    store_c.start()
    halo_wait(2)
    halo_read(2)
    lift(mat_f, jf, qf, ((flinks, tab_h, 128),))
    store_f = pltpu.make_async_copy(qf, outf_hbm, out_sem.at[1])
    store_f.start()

    for phase in range(3):
        for copy in halo_copies(phase):
            copy.wait_send()
        for d in range(1, n_sub):
            exchange_copy(phase, d).wait_send()
    store_c.wait()
    store_f.wait()


def per_device(n_dom, n_sub, coarse, fine, cel, cden, fel, fden, clinks, flinks, csend, fret, selem, samp, sshape):
    hbm = pl.BlockSpec(memory_space=pl.ANY)
    vmem = pl.BlockSpec(memory_space=pltpu.VMEM)
    smem = pl.BlockSpec(memory_space=pltpu.SMEM)
    field = pltpu.VMEM((576, 128), F32)
    faces = pltpu.VMEM((864, 128), F32)
    trace = pltpu.VMEM((144, 128), F32)
    out = jax.ShapeDtypeStruct((576, 128), F32)

    def body(*refs):
        kernel(n_dom, n_sub, *refs)

    c, f = pl.pallas_call(
        body,
        name="lts",
        out_shape=(out, out),
        in_specs=[hbm, hbm] + [vmem] * 8 + [smem, smem, vmem, vmem],
        out_specs=(hbm, hbm),
        scratch_shapes=[field] * 8
        + [pltpu.VMEM((192, 1152), BF16), pltpu.VMEM((192, 1152), F32)]
        + [faces] * 5
        + [trace] * 3
        + [pltpu.VMEM((3, 2, 72, 128), F32)] * 2
        + [pltpu.VMEM((3, 8, 24, 128), F32)] * 2
        + [pltpu.SemaphoreType.DMA((2,))] * 2
        + [pltpu.SemaphoreType.DMA((3, 2))] * 2
        + [pltpu.SemaphoreType.DMA((3, 7))] * 2,
        compiler_params=pltpu.CompilerParams(collective_id=0, has_side_effects=True),
    )(coarse.reshape(576, 128), fine.reshape(576, 128), cel, cden, fel, fden, clinks, flinks, csend, fret,
      selem, samp.T, sshape.T, jnp.asarray(derivative_tables()))
    return c.reshape(9, 64, 128), f.reshape(9, 64, 128)


def solution(mesh):
    n_dom, n_sub = mesh.shape["dom"], mesh.shape["sub"]
    every = ("dom", "sub")

    def body(*args):
        return per_device(n_dom, n_sub, *args)

    return jax.shard_map(
        body,
        mesh=mesh,
        in_specs=(
            P(None, None, every), P(None, None, every), P(None, every), P(every), P(None, every), P(every),
            P(None, every), P(None, every), P(every), P(every), P(every), P(None, every), P(None, every),
        ),
        out_specs=(P(None, None, every), P(None, None, every)),
        check_vma=False,
    )
```

time: 221 us -> 36.8 us (0.17); the launches traced: 218 us -> 36.6 us
  local copies, waits for them, and re-layouts: 120 us -> 2.46 us
  starting transfers between devices: 56.9 us -> 0 us
  Pallas kernels: 0 us -> 33.5 us
  other arithmetic: 20.6 us -> 0 us
  matrix products: 11.2 us -> 0 us
  waiting for transfers between devices: 4.58 us -> 0 us
  between operations: 4.15 us -> 0.65 us
    unnamed x485 -> x4, local copies, waits for them, and re-layouts: 64.1 us -> 2.46 us
    pallas_call x0 -> x1, Pallas kernels: none -> 33.5 us  [per_device(): pl.pallas_call(body, name='lts', out_shape=(out, out), in_specs=[hbm, hbm...]
    all_to_all x3 -> x0, starting transfers between devices: 33.5 us -> none  [the longest x2 19.5 us: per_device(): lax.all_to_all(piece_back, 'sub', split_axis=1, concat_axis=1, tiled=True)]
    gather x42 -> x0, local copies, waits for them, and re-layouts: 27.3 us -> none  [the longest x36 18.3 us: correct(): outer_trace = jnp.take(trace_table, links[face_index], axis=1)]
    ppermute x6 -> x0, starting transfers between devices: 23.4 us -> none  [the longest x3 12.7 us: padded(): lax.ppermute(head, axis, [((i + 1) % count, i) for i in range(count)])]
    another operation x63 -> x0, local copies, waits for them, and re-layouts: 19.8 us -> none  [the longest x42 17.9 us: face_traces(): return [piece.reshape(144, count_elems) for piece in slices]]
    dot_general x13 -> x0, matrix products: 11.2 us -> none  [the longest x12 10.2 us: volume_rate(): jnp.einsum('ygq,kqp->ykgp', lookup_tables, nodal_field, precision=highest...]
    slice x40 -> x0, local copies, waits for them, and re-layouts: 9.24 us -> none  [the longest x9 2.42 us: face_traces(): cube[:, 3]]
  transfers between devices with their start and end apart: 9 -> 0, of which waited for: 1 -> 0; matrix products, arithmetic and copies ran while one was open for 17% -> 0% of each run, Pallas kernels for 0% -> 0%
where the time goes in v1:
time: 36.8 us; the launch traced here: 36.6 us
  Pallas kernels  33.5 us (91%)
  local copies, waits for them, and re-layouts  2.46 us (7%)
  between operations  0.65 us (2%)
    pallas_call x1, Pallas kernels, per_device(): pl.pallas_call(body, name='lts', out_shape=(out, out), in_specs=[hbm, hbm...  33.5 us
    unnamed x4, local copies, waits for them, and re-layouts  2.46 us

profile of v1, /device:TPU:1, one launch (start us, length us, event | category | flops | bytes accessed | tf_op | source)
XLA Modules:
  0.0 36.6 jit_solution(15092897310568858330)
XLA Ops:
  0.6 33.5 %lts.1 = (f32[576,128]{1,0:T(8,128)}, f32[576,128]{1,0:T(8,128)}) custom-call(f32[576,128]{1,0:T(8,128)} %bitcast.6, f32[576,128]{1,0:T(8,128)} %bitcast.7, f32[2,128]{1,0:T(2,128)} %refs_2_.1, f32[128]{0:T(128)} %refs_3_.1, f32[2,128]{1,0:T(2,128)} %refs_4_.1, f32[128]{0:T(128)} %refs_5_.1, s32[6,128]{1,0:T(8,128)} %refs_6_.1, s32[6,128]{1,0:T(8,128)} %refs_7_.1, ...), custom_call_target="tpu_custom_call" | custom-call | tf_op jit(solution)/shard_map/lts/pallas_call | solution.py:369
  34.1 0.0 copy-start
  34.2 1.7 %copy.18 = f32[9,64,128]{2,1,0:T(8,128)} copy(f32[9,64,128]{2,1,0:T(8,128)} %bitcast.9) | data formatting | bytes 589824
  35.9 0.0 copy-done
  35.9 0.7 %copy.19 = f32[9,64,128]{2,1,0:T(8,128)} copy(f32[9,64,128]{2,1,0:T(8,128)S(1)} %bitcast.8) | data formatting | bytes 589824
Async XLA Ops:
  34.1 1.8 %copy-start = (f32[576,128]{1,0:T(8,128)S(1)}, f32[576,128]{1,0:T(8,128)}, u32[]{:S(2)}) copy-start(f32[576,128]{1,0:T(8,128)} %get-tuple-element.5) | copy-start | bytes 884740

commit v2 on v1

--- a/solution.py
+++ b/solution.py
@@ -11,9 +11,9 @@
 MESH = pl.DeviceIdType.MESH
 COARSE_DT = 0.03
 FINE_DT = 0.015
+ORDER = (4, 3, 5, 2, 6, 1, 7)
 F32 = jnp.float32
 BF16 = jnp.bfloat16
-
 
 def derivative_tables():
     points = np.array([-1.0, -1.0 / math.sqrt(5.0), 1.0 / math.sqrt(5.0), 1.0])
@@ -28,17 +28,16 @@
     along_x = np.kron(d, np.eye(16))
     along_y = np.kron(np.kron(eye, d), eye)
     along_z = np.kron(np.eye(16), d)
-    full = np.concatenate([along_x, along_y, along_z]).astype(np.float32)
+    full = np.concatenate([along_x, along_y, along_z, along_x]).astype(np.float32)
     high = full.astype(BF16)
     low = (full - high.astype(np.float32)).astype(BF16)
     return np.concatenate([high, low, high], axis=1)
 
-
 def kernel(n_dom, n_sub, *refs):
-    (qc_hbm, qf_hbm, cel, cden, fel, fden, clinks, flinks, csend, fret, selem, samp, sshape, dmat,
-     outc_hbm, outf_hbm,
-     qc, qf, cur, ic, if_, c0, base_c, base_f, rhs, grads, tc, t0, tf, jc, jf, tab_h, tab_i, ret0,
-     hs, hr, xs, xr, in_sem, out_sem, hs_sem, hr_sem, xs_sem, xr_sem) = refs
+    hbm_refs, (out_c, out_f), vmem_refs = refs[:14], refs[14:16], refs[16:30]
+    (qc, qf, cel, cden, fel, fden, clinks, flinks, csend, fret, selem, samp, sshape, dmat) = vmem_refs
+    (cur, ic, if_, c0, base_f, tc, t0, tf, jc, jf, tab_h, tab_i, ret0,
+     hs, hr, xs, xr, in_sem, hs_sem, hr_sem, xs_sem, xr_sem) = refs[30:]
 
     dom, sub = lax.axis_index("dom"), lax.axis_index("sub")
     n_all = n_dom * n_sub
@@ -47,10 +46,11 @@
     above_id = (above // n_sub, lax.rem(above, n_sub))
     below_id = (below // n_sub, lax.rem(below, n_sub))
 
-    load_f = pltpu.make_async_copy(qf_hbm, qf, in_sem.at[0])
-    load_c = pltpu.make_async_copy(qc_hbm, qc, in_sem.at[1])
-    load_f.start()
-    load_c.start()
+    loads = [pltpu.make_async_copy(src, dst, in_sem.at[i]) for i, (src, dst) in enumerate(zip(hbm_refs, vmem_refs))]
+    early = (1, 4, 5, 13)
+    late = (0, 2, 3, 8, 7, 9, 6, 10, 11, 12)
+    for i in early:
+        loads[i].start()
 
     barrier = pltpu.get_barrier_semaphore()
     for d in range(1, n_sub):
@@ -58,6 +58,9 @@
     for peer in (above_id, below_id):
         pl.semaphore_signal(barrier, inc=1, device_id=peer, device_id_type=MESH)
 
+    for i in late:
+        loads[i].start()
+
     lane = lax.broadcasted_iota(jnp.int32, (1, 128), 1)
     lane_lo = lane < 64
     sub_lo = lax.broadcasted_iota(jnp.int32, (8, 1), 0) < 4
@@ -68,35 +71,31 @@
         speed = jnp.sqrt((lame + 2.0 * shear) * buoy)
         return lame * g, shear * g, buoy * g, speed * g
 
-    mat_c, mat_f = material(cel, cden, 1.0), material(fel, fden, 2.0)
-
     def rates(src, mat, emit):
-        for v in range(9):
+        lame, shear, buoy, _ = mat
+
+        def along(v, first, last):
             x = src[64 * v : 64 * v + 64, :]
             high = x.astype(BF16)
             low = (x - high.astype(F32)).astype(BF16)
-            at = slice(128 * v, 128 * v + 128)
-            rhs[0:64, at] = high
-            rhs[64:128, at] = high
-            rhs[128:192, at] = low
-        grads[...] = jnp.dot(dmat[...], rhs[...], preferred_element_type=F32)
-        lame, shear, buoy, _ = mat
-
-        def gr(axis, v):
-            return grads[64 * axis : 64 * axis + 64, 128 * v : 128 * v + 128]
-
-        x6, y7, z8 = gr(0, 6), gr(1, 7), gr(2, 8)
+            parts = jnp.dot(dmat[64 * first : 64 * last, :], jnp.concatenate([high, high, low], axis=0),
+                            preferred_element_type=F32)
+            return [parts[64 * i : 64 * i + 64, :] for i in range(last - first)]
+
+        (x0,), (y1,), (z2,) = along(0, 0, 1), along(1, 1, 2), along(2, 2, 3)
+        (x3, y3), (y4, z4), (z5, x5) = along(3, 0, 2), along(4, 1, 3), along(5, 2, 4)
+        accel = [buoy * (x0 + y3 + z5), buoy * (x3 + y1 + z4), buoy * (x5 + y4 + z2)]
+        (x6, y6, z6), (x7, y7, z7), (x8, y8, z8) = [along(v, 0, 3) for v in (6, 7, 8)]
         spread = lame * (x6 + y7 + z8)
         shear2 = 2.0 * shear
         emit(0, spread + shear2 * x6)
         emit(1, spread + shear2 * y7)
         emit(2, spread + shear2 * z8)
-        emit(3, shear * (gr(1, 6) + gr(0, 7)))
-        emit(4, shear * (gr(2, 7) + gr(1, 8)))
-        emit(5, shear * (gr(2, 6) + gr(0, 8)))
-        emit(6, buoy * (gr(0, 0) + gr(1, 3) + gr(2, 5)))
-        emit(7, buoy * (gr(0, 3) + gr(1, 1) + gr(2, 4)))
-        emit(8, buoy * (gr(0, 5) + gr(1, 4) + gr(2, 2)))
+        emit(3, shear * (y6 + x7))
+        emit(4, shear * (z7 + y8))
+        emit(5, shear * (z6 + x8))
+        for v in range(3):
+            emit(6 + v, accel[v])
 
     def predictor(src, mat, targets):
         cur[...] = src[...]
@@ -117,6 +116,22 @@
             return weights
 
         lax.fori_loop(0, 3, order, tuple(jnp.float32(dt) for _, dt in targets))
+
+    def nested(src, mat, out, dt):
+        out[...] = src[...]
+
+        def order(k, _):
+            outer = jnp.where(k == 2, dt, 1.0).astype(F32)
+            inner = jnp.where(k == 0, dt / 4.0, jnp.where(k == 1, dt / 3.0, dt * dt / 2.0)).astype(F32)
+
+            def emit(v, value):
+                at = slice(64 * v, 64 * v + 64)
+                out[at, :] = outer * src[at, :] + value
+
+            rates(out, tuple(inner * m for m in mat), emit)
+            return 0
+
+        lax.fori_loop(0, 3, order, 0)
 
     def traces(src, out):
         for v in range(9):
@@ -169,7 +184,7 @@
         parts = butterfly(parts + [parts[0], parts[0]])
         for b in range(8):
             xs[phase, b] = parts[b]
-        for d in range(1, n_sub):
+        for d in ORDER:
             exchange_copy(phase, d).start()
 
     def exchange_wait(phase):
@@ -276,19 +291,24 @@
 
         rates(integral, mat, emit)
 
-    send_row = csend[...].reshape(1, 128)
-    return_row = fret[...].reshape(1, 128)
-
-    load_f.wait()
-    predictor(qf, mat_f, ((if_, FINE_DT),))
+    for i in early:
+        loads[i].wait()
+    mat_f = material(fel, fden, 2.0)
+    nested(qf, mat_f, if_, FINE_DT)
     traces(if_, tf)
+
     halo_pack(0, tf)
     pl.semaphore_wait(barrier, n_sub + 1)
     halo_start(0)
 
-    load_c.wait()
+    for i in late:
+        loads[i].wait()
+    mat_c = material(cel, cden, 1.0)
+    send_row = csend[...].reshape(1, 128)
+    return_row = fret[...].reshape(1, 128)
     predictor(qc, mat_c, ((c0, FINE_DT), (ic, COARSE_DT)))
     traces(c0, t0)
+
     first = face_columns(t0, send_row)
     exchange_start(0, first)
 
@@ -305,28 +325,30 @@
     tab_i[...] = exchange_read(0)
     exchange_start(1, second)
     halo_start(1)
+
     lift(mat_f, jf, base_f, ((flinks, tab_h, 128), (flinks, tab_i, 256)))
 
-    predictor(base_f, mat_f, ((if_, FINE_DT),))
+    nested(base_f, mat_f, if_, FINE_DT)
     traces(if_, tf)
+
     halo_pack(2, tf)
     halo_start(2)
     exchange_start(2, ret0[...] + face_columns(tf, return_row))
 
-    start_base(base_f, if_, mat_f, qf)
+    start_base(base_f, if_, mat_f, out_f)
     jump_own(flinks, tf, jf)
-    start_base(qc, ic, mat_c, base_c)
+    start_base(qc, ic, mat_c, out_c)
     jump_own(clinks, tc, jc)
-    node_of = sshape[...]
-    rows = lax.broadcasted_iota(jnp.int32, (4, 128), 0)
-    lanes = lax.broadcasted_iota(jnp.int32, (4, 128), 1)
+    node_of, amp = sshape[...], COARSE_DT * samp[...]
+    square = lax.broadcasted_iota(jnp.int32, (4, 4), 0) == lax.broadcasted_iota(jnp.int32, (4, 4), 1)
+    spot = selem[...].astype(F32).reshape(1, 4)
+    column = jnp.sum(jnp.where(square, spot, 0.0), axis=1, keepdims=True)
+    hit = lane.astype(F32) == column
     for v in range(9):
-        spots = jnp.zeros((4, 128), F32)
-        for i in range(4):
-            spots = jnp.where((rows == i) & (lanes == selem[i]), COARSE_DT * samp[i, v], spots)
-        field = lax.dot_general(node_of, spots, (((0,), (0,)), ((), ())), precision=lax.Precision.HIGHEST,
-                                preferred_element_type=F32)
-        base_c[64 * v : 64 * v + 64, :] = base_c[64 * v : 64 * v + 64, :] + field
+        field = lax.dot_general(node_of, jnp.where(hit, amp[:, v : v + 1], 0.0), (((0,), (0,)), ((), ())),
+                                precision=lax.Precision.HIGHEST, preferred_element_type=F32)
+        out_c[64 * v : 64 * v + 64, :] = out_c[64 * v : 64 * v + 64, :] + field
+
     exchange_wait(1)
     tab_i[...] = exchange_read(1)
     jump_add(flinks, jf, tab_i, 256)
@@ -334,30 +356,30 @@
     halo_read(1)
     jump_add(clinks, jc, tab_h, 128)
 
+    halo_wait(2)
+    halo_read(2)
+    lift(mat_f, jf, out_f, ((flinks, tab_h, 128),))
+
     exchange_wait(2)
     tab_i[...] = exchange_read(2)
-    lift(mat_c, jc, base_c, ((clinks, tab_i, 256),))
-    store_c = pltpu.make_async_copy(base_c, outc_hbm, out_sem.at[0])
-    store_c.start()
-    halo_wait(2)
-    halo_read(2)
-    lift(mat_f, jf, qf, ((flinks, tab_h, 128),))
-    store_f = pltpu.make_async_copy(qf, outf_hbm, out_sem.at[1])
-    store_f.start()
+    lift(mat_c, jc, out_c, ((clinks, tab_i, 256),))
 
     for phase in range(3):
         for copy in halo_copies(phase):
             copy.wait_send()
-        for d in range(1, n_sub):
+        for d in ORDER:
             exchange_copy(phase, d).wait_send()
-    store_c.wait()
-    store_f.wait()
-
+
+def store(c_ref, f_ref, outc_ref, outf_ref, sem):
+    copies = [pltpu.make_async_copy(src, dst, sem.at[i]) for i, (src, dst) in enumerate(((c_ref, outc_ref), (f_ref, outf_ref)))]
+    for piece in copies:
+        piece.start()
+    for piece in copies:
+        piece.wait()
 
 def per_device(n_dom, n_sub, coarse, fine, cel, cden, fel, fden, clinks, flinks, csend, fret, selem, samp, sshape):
     hbm = pl.BlockSpec(memory_space=pl.ANY)
     vmem = pl.BlockSpec(memory_space=pltpu.VMEM)
-    smem = pl.BlockSpec(memory_space=pltpu.SMEM)
     field = pltpu.VMEM((576, 128), F32)
     faces = pltpu.VMEM((864, 128), F32)
     trace = pltpu.VMEM((144, 128), F32)
@@ -366,26 +388,34 @@
     def body(*refs):
         kernel(n_dom, n_sub, *refs)
 
+    args = (coarse.reshape(576, 128), fine.reshape(576, 128), cel, cden, fel, fden, clinks, flinks, csend, fret,
+            selem, samp.T, sshape.T, jnp.asarray(derivative_tables()))
     c, f = pl.pallas_call(
         body,
         name="lts",
-        out_shape=(out, out),
-        in_specs=[hbm, hbm] + [vmem] * 8 + [smem, smem, vmem, vmem],
-        out_specs=(hbm, hbm),
-        scratch_shapes=[field] * 8
-        + [pltpu.VMEM((192, 1152), BF16), pltpu.VMEM((192, 1152), F32)]
+        out_shape=(pltpu.VMEM((576, 128), F32), pltpu.VMEM((576, 128), F32)),
+        in_specs=[hbm] * 14,
+        out_specs=(vmem, vmem),
+        scratch_shapes=[pltpu.VMEM(a.shape, a.dtype) for a in args]
+        + [field] * 5
         + [faces] * 5
         + [trace] * 3
         + [pltpu.VMEM((3, 2, 72, 128), F32)] * 2
         + [pltpu.VMEM((3, 8, 24, 128), F32)] * 2
-        + [pltpu.SemaphoreType.DMA((2,))] * 2
+        + [pltpu.SemaphoreType.DMA((14,))]
         + [pltpu.SemaphoreType.DMA((3, 2))] * 2
         + [pltpu.SemaphoreType.DMA((3, 7))] * 2,
         compiler_params=pltpu.CompilerParams(collective_id=0, has_side_effects=True),
-    )(coarse.reshape(576, 128), fine.reshape(576, 128), cel, cden, fel, fden, clinks, flinks, csend, fret,
-      selem, samp.T, sshape.T, jnp.asarray(derivative_tables()))
+    )(*args)
+    c, f = pl.pallas_call(
+        store,
+        name="put",
+        out_shape=(out, out),
+        in_specs=[vmem, vmem],
+        out_specs=(hbm, hbm),
+        scratch_shapes=[pltpu.SemaphoreType.DMA((2,))],
+    )(pltpu.with_memory_space_constraint(c, pltpu.VMEM), pltpu.with_memory_space_constraint(f, pltpu.VMEM))
     return c.reshape(9, 64, 128), f.reshape(9, 64, 128)
-
 
 def solution(mesh):
     n_dom, n_sub = mesh.shape["dom"], mesh.shape["sub"]

time: 36.8 us -> 32.8 us (0.89)
  local copies, waits for them, and re-layouts: 2.46 us -> 0 us
  Pallas kernels: 33.5 us -> 32 us
    unnamed x4 -> x0, local copies, waits for them, and re-layouts: 2.46 us -> none
    pallas_call x1 -> x2, Pallas kernels: 33.5 us -> 32 us  [the longest x1 31.2 us: per_device(): pl.pallas_call(body, name='lts', out_shape=(pltpu.VMEM((576, 128), F32),...]
where the time goes in v2:
time: 32.8 us; the launch traced here: 32.6 us
  Pallas kernels  32 us (98%)
  between operations  0.64 us (2%)
    pallas_call x1, Pallas kernels, per_device(): pl.pallas_call(body, name='lts', out_shape=(pltpu.VMEM((576, 128), F32),...  31.2 us
    pallas_call x1, Pallas kernels, per_device(): pl.pallas_call(store, name='put', out_shape=(out, out), in_specs=[vmem, v...  0.83 us

profile of v2, /device:TPU:1, one launch (start us, length us, event | category | flops | bytes accessed | tf_op | source)
XLA Modules:
  0.0 32.6 jit_solution(6847095765272918804)
XLA Ops:
  0.6 31.2 %lts.1 = (f32[576,128]{1,0:T(8,128)S(1)}, f32[576,128]{1,0:T(8,128)S(1)}) custom-call(f32[576,128]{1,0:T(8,128)} %bitcast.6, f32[576,128]{1,0:T(8,128)} %bitcast.7, f32[2,128]{1,0:T(2,128)} %refs_2_.1, f32[128]{0:T(128)} %refs_3_.1, f32[2,128]{1,0:T(2,128)} %refs_4_.1, f32[128]{0:T(128)} %refs_5_.1, s32[6,128]{1,0:T(8,128)} %refs_6_.1, s32[6,128]{1,0:T(8,128)} %refs_7_.1, ...), custom_call_target="tpu_custom_call" | custom-call | tf_op jit(solution)/shard_map/lts/pallas_call | solution.py:393
  31.8 0.8 %put.1 = (f32[576,128]{1,0:T(8,128)}, f32[576,128]{1,0:T(8,128)}) custom-call(f32[576,128]{1,0:T(8,128)S(1)} %get-tuple-element.6.c_ref, f32[576,128]{1,0:T(8,128)S(1)} %get-tuple-element.7.f_ref), custom_call_target="tpu_custom_call" | custom-call | tf_op jit(solution)/shard_map/put/pallas_call | solution.py:410

commit v3 on v2

--- a/solution.py
+++ b/solution.py
@@ -15,7 +15,7 @@
 F32 = jnp.float32
 BF16 = jnp.bfloat16
 
-def derivative_tables():
+def derivative():
     points = np.array([-1.0, -1.0 / math.sqrt(5.0), 1.0 / math.sqrt(5.0), 1.0])
     bary = np.array([1.0 / np.prod([points[c] - points[o] for o in range(4) if o != c]) for c in range(4)])
     d = np.zeros((4, 4))
@@ -24,11 +24,13 @@
             if r != c:
                 d[r, c] = bary[c] / bary[r] / (points[r] - points[c])
         d[r, r] = -np.sum(d[r])
-    eye = np.eye(4)
-    along_x = np.kron(d, np.eye(16))
+    return d
+
+def derivative_tables():
+    d, eye = derivative(), np.eye(4)
     along_y = np.kron(np.kron(eye, d), eye)
     along_z = np.kron(np.eye(16), d)
-    full = np.concatenate([along_x, along_y, along_z, along_x]).astype(np.float32)
+    full = np.concatenate([along_y, along_z]).astype(np.float32)
     high = full.astype(BF16)
     low = (full - high.astype(np.float32)).astype(BF16)
     return np.concatenate([high, low, high], axis=1)
@@ -36,7 +38,7 @@
 def kernel(n_dom, n_sub, *refs):
     hbm_refs, (out_c, out_f), vmem_refs = refs[:14], refs[14:16], refs[16:30]
     (qc, qf, cel, cden, fel, fden, clinks, flinks, csend, fret, selem, samp, sshape, dmat) = vmem_refs
-    (cur, ic, if_, c0, base_f, tc, t0, tf, jc, jf, tab_h, tab_i, ret0,
+    (ic, if_, c0, base_f, tc, t0, tf, jc, jf, tab_h, tab_i, ret0,
      hs, hr, xs, xr, in_sem, hs_sem, hr_sem, xs_sem, xr_sem) = refs[30:]
 
     dom, sub = lax.axis_index("dom"), lax.axis_index("sub")
@@ -46,18 +48,17 @@
     above_id = (above // n_sub, lax.rem(above, n_sub))
     below_id = (below // n_sub, lax.rem(below, n_sub))
 
+    barrier = pltpu.get_barrier_semaphore()
+    for peer in (below_id, above_id):
+        pl.semaphore_signal(barrier, inc=1, device_id=peer, device_id_type=MESH)
+    for d in ORDER:
+        pl.semaphore_signal(barrier, inc=1, device_id=(dom, lax.rem(sub + d, n_sub)), device_id_type=MESH)
+
     loads = [pltpu.make_async_copy(src, dst, in_sem.at[i]) for i, (src, dst) in enumerate(zip(hbm_refs, vmem_refs))]
-    early = (1, 4, 5, 13)
-    late = (0, 2, 3, 8, 7, 9, 6, 10, 11, 12)
+    early = (1, 0, 4, 5, 2, 3, 13)
+    late = (8, 7, 9, 6, 10, 11, 12)
     for i in early:
         loads[i].start()
-
-    barrier = pltpu.get_barrier_semaphore()
-    for d in range(1, n_sub):
-        pl.semaphore_signal(barrier, inc=1, device_id=(dom, lax.rem(sub + d, n_sub)), device_id_type=MESH)
-    for peer in (above_id, below_id):
-        pl.semaphore_signal(barrier, inc=1, device_id=peer, device_id_type=MESH)
-
     for i in late:
         loads[i].start()
 
@@ -71,64 +72,58 @@
         speed = jnp.sqrt((lame + 2.0 * shear) * buoy)
         return lame * g, shear * g, buoy * g, speed * g
 
+    table = derivative()
+
+    def along_x(x):
+        part = [x[16 * i : 16 * i + 16, :] for i in range(4)]
+        out = []
+        for i in range(4):
+            terms = [float(table[i, k]) * part[k] for k in range(4) if abs(table[i, k]) > 1e-9]
+            while len(terms) > 1:
+                terms = [terms[n] + terms[n + 1] if n + 1 < len(terms) else terms[n] for n in range(0, len(terms), 2)]
+            out.append(terms[0])
+        return jnp.concatenate(out, axis=0)
+
+    def split(x):
+        high = x.astype(BF16)
+        low = (x - high.astype(F32)).astype(BF16)
+        return jnp.concatenate([high, high, low], axis=0)
+
+    def along(pair, first, last):
+        both = jnp.concatenate([split(x) for x in pair], axis=1)
+        got = jnp.dot(dmat[64 * first : 64 * last, :], both, preferred_element_type=F32)
+        return [[got[64 * i : 64 * i + 64, 128 * k : 128 * k + 128] for i in range(last - first)] for k in range(2)]
+
     def rates(src, mat, emit):
         lame, shear, buoy, _ = mat
-
-        def along(v, first, last):
-            x = src[64 * v : 64 * v + 64, :]
-            high = x.astype(BF16)
-            low = (x - high.astype(F32)).astype(BF16)
-            parts = jnp.dot(dmat[64 * first : 64 * last, :], jnp.concatenate([high, high, low], axis=0),
-                            preferred_element_type=F32)
-            return [parts[64 * i : 64 * i + 64, :] for i in range(last - first)]
-
-        (x0,), (y1,), (z2,) = along(0, 0, 1), along(1, 1, 2), along(2, 2, 3)
-        (x3, y3), (y4, z4), (z5, x5) = along(3, 0, 2), along(4, 1, 3), along(5, 2, 4)
-        accel = [buoy * (x0 + y3 + z5), buoy * (x3 + y1 + z4), buoy * (x5 + y4 + z2)]
-        (x6, y6, z6), (x7, y7, z7), (x8, y8, z8) = [along(v, 0, 3) for v in (6, 7, 8)]
+        x = [src[64 * v : 64 * v + 64, :] for v in range(9)]
+        (y6, z6), (y7, z7) = along((x[6], x[7]), 0, 2)
+        (y8, z8), (y4, z4) = along((x[8], x[4]), 0, 2)
+        (y3,), (y1,) = along((x[3], x[1]), 0, 1)
+        (z5,), (z2,) = along((x[5], x[2]), 1, 2)
+        x6, x7, x8, x0, x3, x5 = [along_x(x[v]) for v in (6, 7, 8, 0, 3, 5)]
         spread = lame * (x6 + y7 + z8)
         shear2 = 2.0 * shear
-        emit(0, spread + shear2 * x6)
-        emit(1, spread + shear2 * y7)
-        emit(2, spread + shear2 * z8)
-        emit(3, shear * (y6 + x7))
-        emit(4, shear * (z7 + y8))
-        emit(5, shear * (z6 + x8))
-        for v in range(3):
-            emit(6 + v, accel[v])
-
-    def predictor(src, mat, targets):
-        cur[...] = src[...]
-        for ref, dt in targets:
-            ref[...] = src[...] * dt
-
-        def order(k, weights):
-            shrink = jnp.where(k == 0, 1.0 / 2.0, jnp.where(k == 1, 1.0 / 3.0, 1.0 / 4.0)).astype(F32)
-            weights = tuple(w * (shrink * dt) for w, (_, dt) in zip(weights, targets))
-
-            def emit(v, value):
-                at = slice(64 * v, 64 * v + 64)
-                cur[at, :] = value
-                for (ref, _), w in zip(targets, weights):
-                    ref[at, :] = ref[at, :] + w * value
-
-            rates(cur, mat, emit)
-            return weights
-
-        lax.fori_loop(0, 3, order, tuple(jnp.float32(dt) for _, dt in targets))
-
-    def nested(src, mat, out, dt):
-        out[...] = src[...]
+        out = [spread + shear2 * x6, spread + shear2 * y7, spread + shear2 * z8,
+               shear * (y6 + x7), shear * (z7 + y8), shear * (z6 + x8),
+               buoy * (x0 + y3 + z5), buoy * (x3 + y1 + z4), buoy * (x5 + y4 + z2)]
+        for v in range(9):
+            emit(v, out[v])
+
+    def nested(dt, jobs):
+        for src, _, out in jobs:
+            out[...] = src[...]
 
         def order(k, _):
             outer = jnp.where(k == 2, dt, 1.0).astype(F32)
             inner = jnp.where(k == 0, dt / 4.0, jnp.where(k == 1, dt / 3.0, dt * dt / 2.0)).astype(F32)
-
-            def emit(v, value):
-                at = slice(64 * v, 64 * v + 64)
-                out[at, :] = outer * src[at, :] + value
-
-            rates(out, tuple(inner * m for m in mat), emit)
+            for src, mat, out in jobs:
+
+                def emit(v, value, src=src, out=out):
+                    at = slice(64 * v, 64 * v + 64)
+                    out[at, :] = outer * src[at, :] + value
+
+                rates(out, tuple(inner * m for m in mat), emit)
             return 0
 
         lax.fori_loop(0, 3, order, 0)
@@ -176,24 +171,31 @@
         peer = lax.rem(sub + d, n_sub)
         return pltpu.make_async_remote_copy(
             src_ref=xs.at[phase, peer], dst_ref=xr.at[phase, sub],
-            send_sem=xs_sem.at[phase, d - 1], recv_sem=xr_sem.at[phase, d - 1],
+            send_sem=xs_sem.at[phase], recv_sem=xr_sem.at[phase],
             device_id=(dom, peer), device_id_type=MESH)
 
     def exchange_start(phase, value):
+        exchange_pack(phase, value)
+        exchange_send(phase)
+
+    def exchange_pack(phase, value):
         parts = [value[24 * i : 24 * i + 24, :] for i in range(6)]
         parts = butterfly(parts + [parts[0], parts[0]])
         for b in range(8):
             xs[phase, b] = parts[b]
+
+    def exchange_send(phase):
         for d in ORDER:
             exchange_copy(phase, d).start()
 
+    def exchange_all(phase):
+        return pltpu.make_async_remote_copy(
+            src_ref=xs.at[phase, pl.ds(0, n_sub - 1)], dst_ref=xr.at[phase, pl.ds(0, n_sub - 1)],
+            send_sem=xs_sem.at[phase], recv_sem=xr_sem.at[phase],
+            device_id=(dom, lax.rem(sub + 1, n_sub)), device_id_type=MESH)
+
     def exchange_wait(phase):
-        for d in range(1, n_sub):
-            origin = lax.rem(sub + n_sub - d, n_sub)
-            pltpu.make_async_remote_copy(
-                src_ref=xs.at[phase, origin], dst_ref=xr.at[phase, origin],
-                send_sem=xs_sem.at[phase, d - 1], recv_sem=xr_sem.at[phase, d - 1],
-                device_id=(dom, origin), device_id_type=MESH).wait_recv()
+        exchange_all(phase).wait_recv()
 
     def exchange_read(phase):
         xr[phase, sub] = xs[phase, sub]
@@ -204,7 +206,7 @@
         return [
             pltpu.make_async_remote_copy(
                 src_ref=hs.at[phase, way], dst_ref=hr.at[phase, way],
-                send_sem=hs_sem.at[phase, way], recv_sem=hr_sem.at[phase, way],
+                send_sem=hs_sem.at[phase], recv_sem=hr_sem.at[phase],
                 device_id=peer, device_id_type=MESH)
             for way, peer in enumerate((above_id, below_id))]
 
@@ -218,9 +220,13 @@
         for copy in halo_copies(phase):
             copy.start()
 
+    def halo_all(phase):
+        return pltpu.make_async_remote_copy(
+            src_ref=hs.at[phase], dst_ref=hr.at[phase], send_sem=hs_sem.at[phase], recv_sem=hr_sem.at[phase],
+            device_id=above_id, device_id_type=MESH)
+
     def halo_wait(phase):
-        for copy in halo_copies(phase):
-            copy.wait_recv()
+        halo_all(phase).wait_recv()
 
     def halo_read(phase):
         lower, upper = hr[phase, 0], hr[phase, 1]
@@ -248,8 +254,14 @@
         for f in range(6):
             axis, sign = f // 2, 1.0 if f % 2 else -1.0
             jump = face(j, f)
-            for links, table, low in extra:
-                jump = jump + pick(links, f, table[...], low)
+            if len(extra) == 1:
+                (links, table_ref, low), = extra
+                jump = jump + pick(links, f, table_ref[...], low)
+            else:
+                row = flinks[f : f + 1, :]
+                index = row & 127
+                outer = jnp.where(row < 256, gather(tab_h[...], index), gather(tab_i[...], index))
+                jump = jump + jnp.where(row < 128, 0.0, outer)
             part = [jump[16 * v : 16 * v + 16, :] for v in range(9)]
             vel = part[normal[axis]]
             lam_s, full_s, shear_s, buoy_s = sign * lame, sign * full, sign * shear, sign * buoy
@@ -294,27 +306,28 @@
     for i in early:
         loads[i].wait()
     mat_f = material(fel, fden, 2.0)
-    nested(qf, mat_f, if_, FINE_DT)
+    mat_c = material(cel, cden, 1.0)
+    nested(FINE_DT, ((qf, mat_f, if_), (qc, mat_c, c0)))
+
     traces(if_, tf)
-
     halo_pack(0, tf)
+    for i in late:
+        loads[i].wait()
+    send_row = csend[...].reshape(1, 128)
+    return_row = fret[...].reshape(1, 128)
+    traces(c0, t0)
+    first = face_columns(t0, send_row)
+    exchange_pack(0, first)
     pl.semaphore_wait(barrier, n_sub + 1)
     halo_start(0)
-
-    for i in late:
-        loads[i].wait()
-    mat_c = material(cel, cden, 1.0)
-    send_row = csend[...].reshape(1, 128)
-    return_row = fret[...].reshape(1, 128)
-    predictor(qc, mat_c, ((c0, FINE_DT), (ic, COARSE_DT)))
-    traces(c0, t0)
-
-    first = face_columns(t0, send_row)
-    exchange_start(0, first)
-
+    exchange_send(0)
+
+    nested(COARSE_DT, ((qc, mat_c, ic),))
     traces(ic, tc)
     second = face_columns(tc, send_row) - first
     halo_pack(1, tc)
+    exchange_start(1, second)
+    halo_start(1)
     start_base(qf, if_, mat_f, base_f)
     jump_own(flinks, tf, jf)
     ret0[...] = face_columns(tf, return_row)
@@ -323,12 +336,10 @@
     halo_read(0)
     exchange_wait(0)
     tab_i[...] = exchange_read(0)
-    exchange_start(1, second)
-    halo_start(1)
 
     lift(mat_f, jf, base_f, ((flinks, tab_h, 128), (flinks, tab_i, 256)))
 
-    nested(base_f, mat_f, if_, FINE_DT)
+    nested(FINE_DT, ((base_f, mat_f, if_),))
     traces(if_, tf)
 
     halo_pack(2, tf)
@@ -356,6 +367,9 @@
     halo_read(1)
     jump_add(clinks, jc, tab_h, 128)
 
+    for phase in range(3):
+        halo_all(phase).wait_send()
+        exchange_all(phase).wait_send()
     halo_wait(2)
     halo_read(2)
     lift(mat_f, jf, out_f, ((flinks, tab_h, 128),))
@@ -363,12 +377,6 @@
     exchange_wait(2)
     tab_i[...] = exchange_read(2)
     lift(mat_c, jc, out_c, ((clinks, tab_i, 256),))
-
-    for phase in range(3):
-        for copy in halo_copies(phase):
-            copy.wait_send()
-        for d in ORDER:
-            exchange_copy(phase, d).wait_send()
 
 def store(c_ref, f_ref, outc_ref, outf_ref, sem):
     copies = [pltpu.make_async_copy(src, dst, sem.at[i]) for i, (src, dst) in enumerate(((c_ref, outc_ref), (f_ref, outf_ref)))]
@@ -397,14 +405,13 @@
         in_specs=[hbm] * 14,
         out_specs=(vmem, vmem),
         scratch_shapes=[pltpu.VMEM(a.shape, a.dtype) for a in args]
-        + [field] * 5
+        + [field] * 4
         + [faces] * 5
         + [trace] * 3
         + [pltpu.VMEM((3, 2, 72, 128), F32)] * 2
         + [pltpu.VMEM((3, 8, 24, 128), F32)] * 2
         + [pltpu.SemaphoreType.DMA((14,))]
-        + [pltpu.SemaphoreType.DMA((3, 2))] * 2
-        + [pltpu.SemaphoreType.DMA((3, 7))] * 2,
+        + [pltpu.SemaphoreType.DMA((3,))] * 4,
         compiler_params=pltpu.CompilerParams(collective_id=0, has_side_effects=True),
     )(*args)
     c, f = pl.pallas_call(

time: 32.8 us -> 29.9 us (0.912)
  Pallas kernels: 32 us -> 29.1 us
    pallas_call x1, Pallas kernels: 31.2 us -> 28.3 us  [per_device(): pl.pallas_call(body, name='lts', out_shape=(pltpu.VMEM((576, 128), F32),...]
where the time goes in v3:
time: 29.9 us; the launch traced here: 29.7 us
  Pallas kernels  29.1 us (97%)
  between operations  0.64 us (2%)
    pallas_call x1, Pallas kernels, per_device(): pl.pallas_call(body, name='lts', out_shape=(pltpu.VMEM((576, 128), F32),...  28.3 us
    pallas_call x1, Pallas kernels, per_device(): pl.pallas_call(store, name='put', out_shape=(out, out), in_specs=[vmem, v...  0.83 us

profile of v3, /device:TPU:1, one launch (start us, length us, event | category | flops | bytes accessed | tf_op | source)
XLA Modules:
  0.0 29.7 jit_solution(3547530913882821572)
XLA Ops:
  0.6 28.3 %lts.1 = (f32[576,128]{1,0:T(8,128)S(1)}, f32[576,128]{1,0:T(8,128)S(1)}) custom-call(f32[576,128]{1,0:T(8,128)} %bitcast.6, f32[576,128]{1,0:T(8,128)} %bitcast.7, f32[2,128]{1,0:T(2,128)} %refs_2_.1, f32[128]{0:T(128)} %refs_3_.1, f32[2,128]{1,0:T(2,128)} %refs_4_.1, f32[128]{0:T(128)} %refs_5_.1, s32[6,128]{1,0:T(8,128)} %refs_6_.1, s32[6,128]{1,0:T(8,128)} %refs_7_.1, ...), custom_call_target="tpu_custom_call" | custom-call | tf_op jit(solution)/shard_map/lts/pallas_call | solution.py:401
  28.9 0.8 %put.1 = (f32[576,128]{1,0:T(8,128)}, f32[576,128]{1,0:T(8,128)}) custom-call(f32[576,128]{1,0:T(8,128)S(1)} %get-tuple-element.6.c_ref, f32[576,128]{1,0:T(8,128)S(1)} %get-tuple-element.7.f_ref), custom_call_target="tpu_custom_call" | custom-call | tf_op jit(solution)/shard_map/put/pallas_call | solution.py:417

commit v4 on v3

--- a/solution.py
+++ b/solution.py
@@ -14,6 +14,7 @@
 ORDER = (4, 3, 5, 2, 6, 1, 7)
 F32 = jnp.float32
 BF16 = jnp.bfloat16
+
 
 def derivative():
     points = np.array([-1.0, -1.0 / math.sqrt(5.0), 1.0 / math.sqrt(5.0), 1.0])
@@ -26,6 +27,7 @@
         d[r, r] = -np.sum(d[r])
     return d
 
+
 def derivative_tables():
     d, eye = derivative(), np.eye(4)
     along_y = np.kron(np.kron(eye, d), eye)
@@ -35,6 +37,7 @@
     low = (full - high.astype(np.float32)).astype(BF16)
     return np.concatenate([high, low, high], axis=1)
 
+
 def kernel(n_dom, n_sub, *refs):
     hbm_refs, (out_c, out_f), vmem_refs = refs[:14], refs[14:16], refs[16:30]
     (qc, qf, cel, cden, fel, fden, clinks, flinks, csend, fret, selem, samp, sshape, dmat) = vmem_refs
@@ -71,6 +74,7 @@
         buoy = 1.0 / den[...].reshape(1, 128)
         speed = jnp.sqrt((lame + 2.0 * shear) * buoy)
         return lame * g, shear * g, buoy * g, speed * g
+
 
     table = derivative()
 
@@ -171,7 +175,7 @@
         peer = lax.rem(sub + d, n_sub)
         return pltpu.make_async_remote_copy(
             src_ref=xs.at[phase, peer], dst_ref=xr.at[phase, sub],
-            send_sem=xs_sem.at[phase], recv_sem=xr_sem.at[phase],
+            send_sem=xs_sem.at[0], recv_sem=xr_sem.at[phase],
             device_id=(dom, peer), device_id_type=MESH)
 
     def exchange_start(phase, value):
@@ -191,7 +195,7 @@
     def exchange_all(phase):
         return pltpu.make_async_remote_copy(
             src_ref=xs.at[phase, pl.ds(0, n_sub - 1)], dst_ref=xr.at[phase, pl.ds(0, n_sub - 1)],
-            send_sem=xs_sem.at[phase], recv_sem=xr_sem.at[phase],
+            send_sem=xs_sem.at[0], recv_sem=xr_sem.at[phase],
             device_id=(dom, lax.rem(sub + 1, n_sub)), device_id_type=MESH)
 
     def exchange_wait(phase):
@@ -206,7 +210,7 @@
         return [
             pltpu.make_async_remote_copy(
                 src_ref=hs.at[phase, way], dst_ref=hr.at[phase, way],
-                send_sem=hs_sem.at[phase], recv_sem=hr_sem.at[phase],
+                send_sem=hs_sem.at[0], recv_sem=hr_sem.at[phase],
                 device_id=peer, device_id_type=MESH)
             for way, peer in enumerate((above_id, below_id))]
 
@@ -222,7 +226,7 @@
 
     def halo_all(phase):
         return pltpu.make_async_remote_copy(
-            src_ref=hs.at[phase], dst_ref=hr.at[phase], send_sem=hs_sem.at[phase], recv_sem=hr_sem.at[phase],
+            src_ref=hs.at[phase], dst_ref=hr.at[phase], send_sem=hs_sem.at[0], recv_sem=hr_sem.at[phase],
             device_id=above_id, device_id_type=MESH)
 
     def halo_wait(phase):
@@ -303,12 +307,12 @@
 
         rates(integral, mat, emit)
 
+
     for i in early:
         loads[i].wait()
     mat_f = material(fel, fden, 2.0)
     mat_c = material(cel, cden, 1.0)
     nested(FINE_DT, ((qf, mat_f, if_), (qc, mat_c, c0)))
-
     traces(if_, tf)
     halo_pack(0, tf)
     for i in late:
@@ -334,14 +338,12 @@
 
     halo_wait(0)
     halo_read(0)
+    jump_add(flinks, jf, tab_h, 128)
     exchange_wait(0)
     tab_i[...] = exchange_read(0)
-
-    lift(mat_f, jf, base_f, ((flinks, tab_h, 128), (flinks, tab_i, 256)))
-
+    lift(mat_f, jf, base_f, ((flinks, tab_i, 256),))
     nested(FINE_DT, ((base_f, mat_f, if_),))
     traces(if_, tf)
-
     halo_pack(2, tf)
     halo_start(2)
     exchange_start(2, ret0[...] + face_columns(tf, return_row))
@@ -359,7 +361,6 @@
         field = lax.dot_general(node_of, jnp.where(hit, amp[:, v : v + 1], 0.0), (((0,), (0,)), ((), ())),
                                 precision=lax.Precision.HIGHEST, preferred_element_type=F32)
         out_c[64 * v : 64 * v + 64, :] = out_c[64 * v : 64 * v + 64, :] + field
-
     exchange_wait(1)
     tab_i[...] = exchange_read(1)
     jump_add(flinks, jf, tab_i, 256)
@@ -367,16 +368,20 @@
     halo_read(1)
     jump_add(clinks, jc, tab_h, 128)
 
-    for phase in range(3):
-        halo_all(phase).wait_send()
-        exchange_all(phase).wait_send()
+    pltpu.make_async_remote_copy(
+        src_ref=hs, dst_ref=hr, send_sem=hs_sem.at[0], recv_sem=hr_sem.at[0],
+        device_id=above_id, device_id_type=MESH).wait_send()
+    part = pl.ds(0, n_sub - 1)
+    pltpu.make_async_remote_copy(
+        src_ref=xs.at[pl.ds(0, 3), part], dst_ref=xr.at[pl.ds(0, 3), part], send_sem=xs_sem.at[0], recv_sem=xr_sem.at[0],
+        device_id=above_id, device_id_type=MESH).wait_send()
     halo_wait(2)
     halo_read(2)
     lift(mat_f, jf, out_f, ((flinks, tab_h, 128),))
-
     exchange_wait(2)
     tab_i[...] = exchange_read(2)
     lift(mat_c, jc, out_c, ((clinks, tab_i, 256),))
+
 
 def store(c_ref, f_ref, outc_ref, outf_ref, sem):
     copies = [pltpu.make_async_copy(src, dst, sem.at[i]) for i, (src, dst) in enumerate(((c_ref, outc_ref), (f_ref, outf_ref)))]
@@ -384,6 +389,7 @@
         piece.start()
     for piece in copies:
         piece.wait()
+
 
 def per_device(n_dom, n_sub, coarse, fine, cel, cden, fel, fden, clinks, flinks, csend, fret, selem, samp, sshape):
     hbm = pl.BlockSpec(memory_space=pl.ANY)
@@ -411,7 +417,7 @@
         + [pltpu.VMEM((3, 2, 72, 128), F32)] * 2
         + [pltpu.VMEM((3, 8, 24, 128), F32)] * 2
         + [pltpu.SemaphoreType.DMA((14,))]
-        + [pltpu.SemaphoreType.DMA((3,))] * 4,
+        + [pltpu.SemaphoreType.DMA((1,)), pltpu.SemaphoreType.DMA((3,))] * 2,
         compiler_params=pltpu.CompilerParams(collective_id=0, has_side_effects=True),
     )(*args)
     c, f = pl.pallas_call(
@@ -424,6 +430,7 @@
     )(pltpu.with_memory_space_constraint(c, pltpu.VMEM), pltpu.with_memory_space_constraint(f, pltpu.VMEM))
     return c.reshape(9, 64, 128), f.reshape(9, 64, 128)
 
+
 def solution(mesh):
     n_dom, n_sub = mesh.shape["dom"], mesh.shape["sub"]
     every = ("dom", "sub")

time: 29.9 us -> 29.8 us (level)
  no operation moved by 1% of the time
where the time goes in v4:
time: 29.8 us; the launch traced here: 29.7 us
  Pallas kernels  29 us (97%)
  between operations  0.64 us (2%)
    pallas_call x1, Pallas kernels, per_device(): pl.pallas_call(body, name='lts', out_shape=(pltpu.VMEM((576, 128), F32),...  28.2 us
    pallas_call x1, Pallas kernels, per_device(): pl.pallas_call(store, name='put', out_shape=(out, out), in_specs=[vmem, v...  0.83 us

profile of v4, /device:TPU:1, one launch (start us, length us, event | category | flops | bytes accessed | tf_op | source)
XLA Modules:
  0.0 29.7 jit_solution(2379322161638017715)
XLA Ops:
  0.6 28.2 %lts.1 = (f32[576,128]{1,0:T(8,128)S(1)}, f32[576,128]{1,0:T(8,128)S(1)}) custom-call(f32[576,128]{1,0:T(8,128)} %bitcast.6, f32[576,128]{1,0:T(8,128)} %bitcast.7, f32[2,128]{1,0:T(2,128)} %refs_2_.1, f32[128]{0:T(128)} %refs_3_.1, f32[2,128]{1,0:T(2,128)} %refs_4_.1, f32[128]{0:T(128)} %refs_5_.1, s32[6,128]{1,0:T(8,128)} %refs_6_.1, s32[6,128]{1,0:T(8,128)} %refs_7_.1, ...), custom_call_target="tpu_custom_call" | custom-call | tf_op jit(solution)/shard_map/lts/pallas_call | solution.py:407
  28.8 0.8 %put.1 = (f32[576,128]{1,0:T(8,128)}, f32[576,128]{1,0:T(8,128)}) custom-call(f32[576,128]{1,0:T(8,128)S(1)} %get-tuple-element.6.c_ref, f32[576,128]{1,0:T(8,128)S(1)} %get-tuple-element.7.f_ref), custom_call_target="tpu_custom_call" | custom-call | tf_op jit(solution)/shard_map/put/pallas_call | solution.py:423
